TPU v7x, 32 devices: a whole 2x2x4 slice. The times are simulated.
32 devices in a mesh: groups: 2 (over y), expert: 4 (over x, core), hidden: 4 (over z).
Axes of the slice: x: 2, y: 2, z: 4, core: 2. Of those that a mesh axis runs over, the one named last changes fastest.
Arguments:
- tokens: bfloat16 [1024, 3072], P(('groups', 'expert'), 'hidden'), parts along dimension 0, may hold values from -6 to 6
- routes: int32 [1024, 2], P(('groups', 'expert')), parts along dimension 0, may hold values from 0 to 7, all different within a row; in each aligned block of 128 rows (0 to 127, 128 to 255, ...) at most 48 rows name the same one
- router_weight: bfloat16 [3072, 8], replicated, may hold values from -0.109375 to 0.109375
- gate_weight: bfloat16 [8, 3072, 8192], P('expert', None, 'hidden'), may hold values from -0.109375 to 0.109375
- up_weight: bfloat16 [8, 3072, 8192], P('expert', None, 'hidden'), may hold values from -0.109375 to 0.109375
- down_weight: bfloat16 [8, 8192, 3072], P('expert', 'hidden'), may hold values from -0.09375 to 0.09375
Outputs:
- mixed: bfloat16 [1024, 3072], P(('groups', 'expert'), 'hidden'), parts along dimension 0
There are 2 independent parts, one for each index of `groups`. A program takes and returns all parts, laid end to end along the dimension named above; an argument that names none is the same for every part. Nothing has to cross between parts.
Inputs may be any that keep to these rules, and one draw needn't show every extreme that they name: `routes`: each token names two different experts. Among the 128 tokens of one index of expert (aligned blocks of rows) no expert is named more than 48 times, a bound that some block reaches.
All inputs are finite; a program needn't handle non-finite values.
Results may differ from a plain program's by a relative error of at most 0.0057.
Values may be sent and summed in bfloat16 or wider, within the bound.
No kernel may reach another device: no remote copies, remote signals or barrier semaphores. Data moves between devices by JAX's collectives and lax.ppermute only.
A program may use at most 128 MiB of HBM per device.

v0:
```python
import jax
import jax.numpy as jnp
from jax import lax
from jax.sharding import PartitionSpec as P

CAP = 48


def per_device(tokens, routes, router_weight, gate_weight, up_weight, down_weight):
    experts_here = gate_weight.shape[0]
    groups = lax.axis_size("expert")
    experts_all = experts_here * groups
    local_tokens = tokens.shape[0]
    capacity = CAP
    flat_ids = routes.reshape(-1)
    onehot = (flat_ids[:, None] == jnp.arange(experts_all, dtype=jnp.int32)[None, :]).astype(
        jnp.int32
    )
    position = jnp.sum((jnp.cumsum(onehot, axis=0) - onehot) * onehot, axis=1)
    slot_of = flat_ids * capacity + position
    owners = jnp.arange(flat_ids.shape[0], dtype=jnp.int32) // 2
    inverse = jnp.full((experts_all * capacity,), local_tokens, jnp.int32).at[slot_of].set(owners)
    gathered = lax.all_gather(tokens, "hidden", axis=1, tiled=True)
    logits = jnp.dot(gathered, router_weight, preferred_element_type=jnp.float32)
    padded = jnp.concatenate([gathered, jnp.zeros((1, gathered.shape[1]), jnp.bfloat16)], axis=0)
    send_rows = padded[inverse].reshape(experts_all, 1, capacity, gathered.shape[1])
    arrived = lax.all_to_all(send_rows, "expert", split_axis=0, concat_axis=1, tiled=True)
    gate_act = jnp.einsum(
        "ensd,edf->ensf", arrived, gate_weight, preferred_element_type=jnp.float32
    )
    up_act = jnp.einsum("ensd,edf->ensf", arrived, up_weight, preferred_element_type=jnp.float32)
    hidden_act = (jax.nn.silu(gate_act) * up_act).astype(jnp.bfloat16)
    hidden_act = hidden_act.reshape(experts_here, groups * capacity, hidden_act.shape[3])
    partial_value = jnp.einsum(
        "erf,efd->erd", hidden_act, down_weight, preferred_element_type=jnp.float32
    )
    summed = lax.psum_scatter(partial_value, "hidden", scatter_dimension=2, tiled=True).astype(
        jnp.bfloat16
    )
    summed = summed.reshape(experts_here, groups, capacity, summed.shape[2])
    returned = lax.all_to_all(summed, "expert", split_axis=1, concat_axis=0, tiled=True)
    results = returned.reshape(experts_all * capacity, returned.shape[3])
    selected = jnp.take_along_axis(logits, routes, axis=1)
    share = jax.nn.sigmoid(selected[:, 0] - selected[:, 1])
    slot_pairs = slot_of.reshape(local_tokens, 2)
    first_out = results[slot_pairs[:, 0]].astype(jnp.float32)
    second_out = results[slot_pairs[:, 1]].astype(jnp.float32)
    mixture = share[:, None] * first_out + (1.0 - share)[:, None] * second_out
    return mixture.astype(jnp.bfloat16)


def solution(mesh):
    return jax.shard_map(
        per_device,
        mesh=mesh,
        in_specs=(
            P(("groups", "expert"), "hidden"),
            P(("groups", "expert"), None),
            P(),
            P("expert", None, "hidden"),
            P("expert", None, "hidden"),
            P("expert", "hidden", None),
        ),
        out_specs=P(("groups", "expert"), "hidden"),
        check_vma=False,
    )
```

profile of v0, /device:TPU:0, one launch (start us, length us, event | category | flops | bytes accessed | tf_op | source)
XLA Modules:
  0.0 209.8 jit_solution(10546477326377145028)
XLA Ops:
  6.5 0.8 copy.41
  7.3 0.1 eq.29
  7.5 0.1 eq.25
  7.6 0.6 reduce-window.6
  8.2 0.2 slice_reduce_fusion
  8.5 0.1 fusion.13
  8.6 0.1 reduce_sum.15
  8.7 0.1 mul.51
  8.9 1.4 scatter_custom_fusion
  10.3 21.5 %all_gather.3 = bf16[128,3072]{1,0:T(8,128)(2,1)S(1)} all-gather(bf16[128,768]{1,0:T(8,128)(2,1)} %param.6), channel_id=1, replica_groups=mesh['groups'=2,'expert'=4,'hidden'=4] {'hidden'}, dimensions={1}, use_global_device_ids=true | all-gather | bytes 983040 | tf_op jit(solution)/shard_map/all_gather | solution.py:23
  31.8 0.9 copy-done.1
  32.8 2.9 %gather_fusion = bf16[384,3072]{1,0:T(8,128)(2,1)S(1)} fusion(bf16[129,3072]{1,0:T(8,128)(2,1)S(1)} %concatenate.3, s32[1024]{0:T(1024)S(1)} %pad_clamp_fusion.2), kind=kCustom, calls=%fused_computation | custom fusion | bytes 4720128 | tf_op jit(solution)/shard_map/gather | solution.py:26
  35.7 31.0 %all_to_all.33 = bf16[8,1,48,3072]{3,2,1,0:T(8,128)(2,1)S(1)} all-to-all(bf16[8,1,48,3072]{3,2,1,0:T(8,128)(2,1)S(1)} %bitcast.57), channel_id=1, replica_groups=mesh['groups'=2,'expert'=4,'hidden'=4] {'expert'}, dimensions={0} | all-to-all | bytes 4718592 | tf_op jit(solution)/shard_map/all_to_all | solution.py:27
  66.7 10.8 %fusion.2 = f32[2,4,48,2048]{3,2,1,0:T(8,128)S(1)} fusion(bf16[2,3072,2048]{2,1,0:T(8,128)(2,1)} %param.9, bf16[4,2,1,48,3072]{4,3,1,0,2:T(8,128)(2,1)S(1)} %bitcast.52), kind=kOutput, calls=%fused_computation.7 | convolution fusion | flops 4831838208 | bytes 30670848 | tf_op jit(solution)/shard_map/ensd,edf->ensf/dot_general | solution.py:28
  77.5 11.0 %multiply_convert_fusion = bf16[2,4,48,2048]{3,2,1,0:T(8,128)(2,1)S(1)} fusion(f32[2,4,48,2048]{3,2,1,0:T(8,128)S(1)} %fusion.2, bf16[2,3072,2048]{2,1,0:T(8,128)(2,1)} %param.10, bf16[4,2,1,48,3072]{4,3,1,0,2:T(8,128)(2,1)S(1)} %bitcast.53), kind=kOutput, calls=%fused_computation.9 | convolution fusion | flops 4836556800 | bytes 32243712 | tf_op jit(solution)/shard_map/ensd,edf->ensf/dot_general | solution.py:31
  88.5 12.9 %fusion.19 = f32[2,192,3072]{2,1,0:T(8,128)} fusion(bf16[2,192,2048]{2,1,0:T(8,128)(2,1)S(1)} %bitcast.56, bf16[2,2048,3072]{2,1,0:T(8,128)(2,1)} %param.11), kind=kOutput, calls=%fused_computation.45 | convolution fusion | flops 4831838208 | bytes 31457280 | tf_op jit(solution)/shard_map/erf,efd->erd/dot_general | solution.py:34
  101.5 0.7 copy-done.3
  102.1 0.1 copy.39
  102.2 0.1 reshape.100
  102.4 0.2 copy-done.2
  102.6 0.3 fusion.18
  102.9 1.4 gather_fusion.3
  104.3 0.1 reshape.103
  104.5 0.2 fusion.10
  104.7 80.6 %reduce-scatter.2.cloned.1.call-done = f32[2,192,768]{2,1,0:T(8,128)} async-done(((f32[2,192,3072]{2,1,0:T(8,128)}), f32[2,192,768]{2,1,0:T(8,128)}) %reduce-scatter.2.cloned.1.call-update) | async-done | bytes 1179664 | tf_op jit(solution)/shard_map/reduce_scatter | solution.py:37
  185.3 1.3 convert_element_type.25
  186.6 0.8 copy.46
  187.5 3.5 %all-to-all-start.1 = ((bf16[2,4,48,768]{3,2,0,1:T(8,128)(2,1)}), bf16[2,4,48,768]{3,2,0,1:T(8,128)(2,1)S(1)}, u32[]{:S(2)}, u32[]{:S(2)}) async-start(bf16[2,4,48,768]{3,2,0,1:T(8,128)(2,1)} %copy.46), calls=%async_computation.2 | async-start | bytes 1179648 | tf_op jit(solution)/shard_map/all_to_all | solution.py:41
  191.0 9.5 %all-to-all-done.1 = bf16[2,4,48,768]{3,2,0,1:T(8,128)(2,1)S(1)} async-done(((bf16[2,4,48,768]{3,2,0,1:T(8,128)(2,1)}), bf16[2,4,48,768]{3,2,0,1:T(8,128)(2,1)S(1)}, u32[]{:S(2)}, u32[]{:S(2)}) %all-to-all-start.1) | async-done | bytes 589856 | tf_op jit(solution)/shard_map/all_to_all | solution.py:41
  200.4 0.9 gather_fusion.2
  201.3 0.9 gather_fusion.1
  202.2 0.8 add_convert_fusion
  (21 shorter events, 0.3 us)
Async XLA Ops:
  6.5 95.8 %copy-start = (bf16[3072,8]{0,1:T(8,128)(2,1)S(1)}, bf16[3072,8]{0,1:T(8,128)(2,1)}, u32[]{:S(2)}) copy-start(bf16[3072,8]{0,1:T(8,128)(2,1)} %param.8) | copy-start | bytes 147460
  6.5 178.8 %reduce-scatter.2.cloned.1.call-start = ((), (), s32[]{:S(2)}) async-start(), calls=%async_computation.3 | async-start | bytes 5898240 | tf_op jit(solution)/shard_map/reduce_scatter | solution.py:37
  31.8 0.9 copy-start.1
  101.4 0.7 copy-start.3
  101.4 1.1 copy-start.2
  187.5 13.0 %all-to-all-start.1 = ((bf16[2,4,48,768]{3,2,0,1:T(8,128)(2,1)}), bf16[2,4,48,768]{3,2,0,1:T(8,128)(2,1)S(1)}, u32[]{:S(2)}, u32[]{:S(2)}) async-start(bf16[2,4,48,768]{3,2,0,1:T(8,128)(2,1)} %copy.46), calls=%async_computation.2 | async-start | bytes 1179648 | tf_op jit(solution)/shard_map/all_to_all | solution.py:41
Sparse Core Ops, SparseCore 0:
  101.6 83.6 reduce-scatter.1
where the time goes:
time: 210 us
  waiting for transfers between devices  90.1 us (43%)
  blocking collectives  52.6 us (25%)
  matrix products  35 us (17%)
  between operations  13.6 us (6%)
  local copies, waits for them, and re-layouts  12.1 us (6%)
  starting transfers between devices  3.48 us (2%)
  other arithmetic  3.13 us (1%)
    reduce_scatter x1, waiting for transfers between devices, per_device(): lax.psum_scatter(partial_value, 'hidden', scatter_dimension=2, tiled=True)  80.6 us
    all_to_all x1, blocking collectives, per_device(): lax.all_to_all(send_rows, 'expert', split_axis=0, concat_axis=1, tiled=True)  31 us
    all_gather x1, blocking collectives, per_device(): gathered = lax.all_gather(tokens, 'hidden', axis=1, tiled=True)  21.5 us
    dot_general x1, matrix products, per_device(): jnp.einsum('erf,efd->erd', hidden_act, down_weight, preferred_element_typ...  12.9 us
    dot_general x1, matrix products, per_device(): jnp.einsum('ensd,edf->ensf', arrived, up_weight, preferred_element_type=j...  11 us
    dot_general x1, matrix products, per_device(): jnp.einsum('ensd,edf->ensf', arrived, gate_weight, preferred_element_type...  10.8 us
    all_to_all x1, waiting for transfers between devices, per_device(): lax.all_to_all(summed, 'expert', split_axis=1, concat_axis=0, tiled=True)  9.45 us
  transfers between devices with their start and end apart: 2, of which 2 were waited for; matrix products, arithmetic and copies ran while one was open for 1% of the time, Pallas kernels for 0%

commit v1 on v0

v1 whole, which is shorter than its diff:
```python
import functools
import jax
import jax.numpy as jnp
from jax import lax
from jax.experimental import pallas as pl
from jax.experimental.pallas import tpu as pltpu
from jax.sharding import PartitionSpec as P


CAP = 48
f32, bf16 = jnp.float32, jnp.bfloat16
VM = pl.BlockSpec(memory_space=pltpu.VMEM)
ANY = pl.BlockSpec(memory_space=pltpu.HBM)
SM = pl.BlockSpec(memory_space=pltpu.SMEM)


def silu_mul(gate, up):
    return (jax.nn.silu(gate) * up).astype(bf16)


def plan_kernel(blocks, experts, idx, *refs):
    names, (sel_out, back_out, sign_out) = refs[:blocks], refs[blocks:]
    toks = names[0].shape[1]
    ahead = (lax.broadcasted_iota(jnp.int32, (toks, toks), 1) < lax.broadcasted_iota(jnp.int32, (toks, toks), 0)).astype(bf16)
    row = lax.broadcasted_iota(jnp.int32, (CAP, toks), 0)
    col = lax.broadcasted_iota(jnp.int32, (toks, CAP), 1)
    num = lax.broadcasted_iota(jnp.int32, (sign_out.shape[2], toks), 0)
    contract = (((1,), (1,)), ((), ()))
    for j in range(blocks):
        pair = names[j][...]
        for e in range(experts):
            own = idx[0] + e
            mine = (pair[0:1] == own) | (pair[1:2] == own)
            flag = mine.astype(f32)
            wide = jnp.broadcast_to(flag, (8, toks)).astype(bf16)
            rank = lax.dot_general(wide, ahead, contract, preferred_element_type=f32)[0:1]
            rank = jnp.where(mine, rank, -1.0).astype(jnp.int32)
            sel_out[j, e * CAP : (e + 1) * CAP] = (rank == row).astype(f32).astype(bf16)
            deep = lax.dot_general(ahead, wide, contract, preferred_element_type=f32)[:, 0:1]
            eye = (lax.broadcasted_iota(jnp.int32, (toks, toks), 1) == lax.broadcasted_iota(jnp.int32, (toks, toks), 0)).astype(bf16)
            held = lax.dot_general(eye, wide, contract, preferred_element_type=f32)[:, 0:1]
            deep = jnp.where(held > 0.5, deep, -1.0).astype(jnp.int32)
            back_out[j, :, e * CAP : (e + 1) * CAP] = (deep == col).astype(f32).astype(bf16)
            other = pair[0:1] + pair[1:2] - own
            sign_out[j, e] = (num == own).astype(f32) - (num == other).astype(f32)


def plan(base, names, experts, count):
    blocks, toks = len(names), names[0].shape[1]
    return pl.pallas_call(
        functools.partial(plan_kernel, blocks, experts),
        out_shape=(
            jax.ShapeDtypeStruct((blocks, experts * CAP, toks), bf16),
            jax.ShapeDtypeStruct((blocks, toks, experts * CAP), bf16),
            jax.ShapeDtypeStruct((blocks, experts, count, toks), f32),
        ),
        in_specs=[SM] + [VM] * blocks,
        out_specs=(VM, VM, VM),
        compiler_params=pltpu.CompilerParams(vmem_limit_bytes=4 << 20),
        cost_estimate=pl.CostEstimate(flops=1 << 24, bytes_accessed=1 << 18, transcendentals=0),
    )(base.reshape(1).astype(jnp.int32), *names)


def plan_plain(base, names, experts, count):
    names = jnp.stack(names)
    blocks, _, toks = names.shape
    here = base + jnp.arange(experts, dtype=jnp.int32)
    mine = (names[:, None, :, :] == here[None, :, None, None]).any(axis=2)
    before = (jnp.arange(toks)[:, None] < jnp.arange(toks)[None, :]).astype(bf16)
    rank = jnp.dot(mine.astype(bf16).reshape(blocks * experts, toks), before, preferred_element_type=f32)
    rank = rank.astype(jnp.int32).reshape(blocks, experts, 1, toks)
    sel = mine[:, :, None, :] & (rank == jnp.arange(CAP, dtype=jnp.int32)[None, None, :, None])
    sel = sel.astype(bf16).reshape(blocks, experts * CAP, toks)
    num = jnp.arange(count, dtype=jnp.int32)[None, None, :, None]
    own = here[None, :, None, None]
    other = jnp.sum(names, axis=1)[:, None, None, :] - own
    return sel, sel.swapaxes(1, 2), (num == own).astype(f32) - (num == other).astype(f32)


def fetch_up(wg, wu, block, kb, out, sem):
    at = pl.ds(pl.multiple_of(block * kb, 128), kb)
    copies = []
    for e in range(wg.shape[0]):
        for m, w in enumerate((wg, wu)):
            copies.append(pltpu.make_async_copy(w.at[e, at], out.at[e, m], sem.at[e, m]))
    return copies


def fetch_down(wd, block, kb, out, sem):
    col = pl.ds(pl.multiple_of(block * kb, 128), kb)
    half = wd.shape[1] // 2
    copies = []
    for e in range(wd.shape[0]):
        for p in range(2):
            rows = pl.ds(p * half, half)
            copies.append(pltpu.make_async_copy(wd.at[e, rows, col], out.at[e, rows], sem.at[e, p]))
    return copies


def first_kernel(idx, tokens, router, wg, wu, tok_out, router_out, w_out, sem, small):
    copies = [
        pltpu.make_async_copy(tokens, tok_out, small.at[0]),
        pltpu.make_async_copy(router, router_out, small.at[1]),
    ] + fetch_up(wg, wu, idx[0], tokens.shape[1], w_out, sem)
    for c in copies:
        c.start()
    for c in copies:
        c.wait()


def first_fetch(block, tokens, router, wg, wu):
    experts, _, ff = wg.shape
    kb = tokens.shape[1]
    return pl.pallas_call(
        first_kernel,
        out_shape=(
            jax.ShapeDtypeStruct(tokens.shape, bf16),
            jax.ShapeDtypeStruct(router.shape, bf16),
            jax.ShapeDtypeStruct((experts, 2, kb, ff), bf16),
        ),
        in_specs=[SM, ANY, ANY, ANY, ANY],
        out_specs=(VM, VM, VM),
        scratch_shapes=[pltpu.SemaphoreType.DMA((experts, 2)), pltpu.SemaphoreType.DMA((2,))],
        compiler_params=pltpu.CompilerParams(vmem_limit_bytes=1 << 20),
        cost_estimate=pl.CostEstimate(flops=0, bytes_accessed=4 * experts * kb * ff, transcendentals=0),
    )(block.reshape(1).astype(jnp.int32), tokens, router, wg, wu)


def up_kernel(first, last, blocks, experts, *refs):
    idx, refs = refs[0], list(refs[1:])
    xs, refs = refs[:blocks], refs[blocks:]
    sel, router, now = refs[:3]
    ahead = refs[3:4] if last else refs[3:5]
    refs = refs[4:] if last else refs[5:]
    if not first:
        g_in, u_in, l_in = refs[:3]
        refs = refs[3:]
    if last:
        sign, h_out, s_out, w_out = refs[:4]
        refs = refs[4:]
    else:
        g_out, u_out, l_out, w_out = refs[:4]
        refs = refs[4:]
    rows, sem = refs
    kb = rows.shape[2]
    fetch = fetch_down if last else fetch_up
    copies = fetch(*ahead, idx[1], kb, w_out, sem)
    for c in copies:
        c.start()
    rt = router[:, pl.ds(pl.multiple_of(idx[0] * kb, 128), kb)]
    for j in range(blocks):
        x = xs[j][...]
        got = jnp.dot(sel[j], x, preferred_element_type=f32).astype(bf16)
        for e in range(experts):
            rows[e, j * CAP : (j + 1) * CAP] = got[e * CAP : (e + 1) * CAP]
        lt = lax.dot_general(rt, x, (((1,), (1,)), ((), ())), preferred_element_type=f32)
        lt = lt if first else l_in[j] + lt
        if not last:
            l_out[j] = lt
            continue
        for e in range(experts):
            w = jax.nn.sigmoid(jnp.sum(sign[j, e] * lt, axis=0, keepdims=True))
            at = sel[j, e * CAP : (e + 1) * CAP].astype(f32)
            s_out[e, j * CAP : (j + 1) * CAP] = jnp.sum(at * w, axis=1, keepdims=True)
    n_all = now.shape[3]
    step = min(512, n_all)

    def column(i, carry):
        e = i // (n_all // step)
        sl = pl.ds(pl.multiple_of(i % (n_all // step) * step, step), step)
        x = rows[e]
        g = jnp.dot(x, now[e, 0, :, sl], preferred_element_type=f32)
        u = jnp.dot(x, now[e, 1, :, sl], preferred_element_type=f32)
        if not first:
            g = g_in[e, :, sl] + g
            u = u_in[e, :, sl] + u
        if last:
            h_out[e, :, sl] = silu_mul(g, u)
        else:
            g_out[e, :, sl] = g
            u_out[e, :, sl] = u
        return carry

    lax.fori_loop(0, experts * (n_all // step), column, 0)
    for c in copies:
        c.wait()


def up_chunk(block, after, xs, sel, sign, router, now, ahead, acc, last):
    experts, _, kb, ff = now.shape
    blocks = len(xs)
    slots = blocks * CAP
    first = acc is None
    big = jax.ShapeDtypeStruct((experts, slots, ff), f32)
    lo = jax.ShapeDtypeStruct((blocks, router.shape[0], xs[0].shape[0]), f32)
    if last:
        out = (
            jax.ShapeDtypeStruct((experts, slots, ff), bf16),
            jax.ShapeDtypeStruct((experts, slots, 1), f32),
            jax.ShapeDtypeStruct((experts, ff, kb), bf16),
        )
    else:
        out = (big, big, lo, jax.ShapeDtypeStruct(now.shape, bf16))
    idx = jnp.stack([block, after]).astype(jnp.int32)
    args = [idx, *xs, sel, router, now, *ahead] + ([] if first else list(acc)) + ([sign] if last else [])
    n0 = 1 + blocks + 3 + len(ahead)
    alias = {} if first or last else {n0: 0, n0 + 1: 1, n0 + 2: 2}
    return pl.pallas_call(
        functools.partial(up_kernel, first, last, blocks, experts),
        out_shape=out,
        in_specs=[SM] + [VM] * blocks + [VM] * 3 + [ANY] * len(ahead) + ([] if first else [VM] * 3) + ([VM] if last else []),
        out_specs=tuple([VM] * len(out)),
        scratch_shapes=[pltpu.VMEM((experts, slots, kb), bf16), pltpu.SemaphoreType.DMA((experts, 2))],
        input_output_aliases=alias,
        compiler_params=pltpu.CompilerParams(vmem_limit_bytes=2 << 20),
        cost_estimate=pl.CostEstimate(
            flops=4 * experts * slots * kb * ff,
            bytes_accessed=4 * experts * kb * ff,
            transcendentals=experts * slots * ff if last else 0,
        ),
    )(*args)


def up_chunk_plain(block, xs, sel, sign, router, wg, wu, acc, last):
    kb, experts, blocks = xs[0].shape[1], wg.shape[0], len(xs)
    x = jnp.stack(xs)
    rows = jnp.einsum("jst,jtd->jsd", sel, x, preferred_element_type=f32).astype(bf16)
    rows = rows.reshape(blocks, experts, CAP, kb).swapaxes(0, 1).reshape(experts, blocks * CAP, kb)
    cut = lambda w: lax.dynamic_slice_in_dim(w, block * kb, kb, axis=1)
    g = jnp.einsum("erd,edf->erf", rows, cut(wg), preferred_element_type=f32)
    u = jnp.einsum("erd,edf->erf", rows, cut(wu), preferred_element_type=f32)
    lo = jnp.einsum("nd,jtd->jnt", cut(router), x, preferred_element_type=f32)
    if acc is not None:
        g, u, lo = g + acc[0], u + acc[1], lo + acc[2]
    if not last:
        return g, u, lo
    weight = jax.nn.sigmoid(jnp.sum(sign * lo[:, None], axis=2))
    at = sel.astype(f32).reshape(blocks, experts, CAP, -1)
    wslot = jnp.sum(at * weight[:, :, None, :], axis=3).swapaxes(0, 1)
    return silu_mul(g, u), wslot.reshape(experts, blocks * CAP, 1)


def down_kernel(experts, blocks, last, *refs):
    idx, h_ref, back, wslot, now, _ = refs[:6]
    if last:
        keep, send, part = refs[6:]
        copies = []
    else:
        wd, keep, send, w_out, part, sem = refs[6:]
        copies = fetch_down(wd, idx[0], part.shape[2], w_out, sem)
    for c in copies:
        c.start()

    def product(e, carry):
        v = jnp.dot(h_ref[e], now[e], preferred_element_type=f32)
        v = (v * wslot[e]).astype(bf16)
        at = pl.ds(pl.multiple_of(e * CAP, CAP), CAP)
        for j in range(blocks):
            part[j, at] = v[j * CAP : (j + 1) * CAP]
        return carry

    lax.fori_loop(0, experts, product, 0)
    for j in range(blocks):
        y = jnp.dot(back[j], part[j], preferred_element_type=f32).astype(bf16)
        if j % 2 == 0:
            keep[j // 2] = y
        else:
            send[j // 2] = y
    for c in copies:
        c.wait()


def down_chunk(after, h, back, wslot, now, wd, gate):
    experts, slots, ff = h.shape
    blocks, toks, _ = back.shape
    kb = now.shape[2]
    last = after is None
    out = (jax.ShapeDtypeStruct((blocks // 2, toks, kb), bf16),) * 2
    args = [jnp.zeros((1,), jnp.int32) if last else after.reshape(1).astype(jnp.int32), h, back, wslot, now, gate]
    return pl.pallas_call(
        functools.partial(down_kernel, experts, blocks, last),
        out_shape=out if last else out + (jax.ShapeDtypeStruct(now.shape, bf16),),
        in_specs=[SM, VM, VM, VM, VM, VM] + ([] if last else [ANY]),
        out_specs=(VM, VM) if last else (VM, VM, VM),
        scratch_shapes=[pltpu.VMEM((blocks, experts * CAP, kb), bf16)]
        + ([] if last else [pltpu.SemaphoreType.DMA((experts, 2))]),
        compiler_params=pltpu.CompilerParams(vmem_limit_bytes=2 << 20),
        cost_estimate=pl.CostEstimate(
            flops=2 * experts * slots * kb * ff, bytes_accessed=2 * experts * kb * ff, transcendentals=0
        ),
    )(*args, *([] if last else [wd]))


def pair_kernel(chips, keep, got, base, *outs):
    for d in range(chips):
        v = keep[d].astype(f32) + got[d].astype(f32)
        if d == 0:
            base[...] = v
        else:
            outs[d - 1][...] = v.astype(bf16)


def pair_sum(keep, got):
    chips, toks, kb = keep.shape
    return pl.pallas_call(
        functools.partial(pair_kernel, chips),
        out_shape=(jax.ShapeDtypeStruct((toks, kb), f32),) + (jax.ShapeDtypeStruct((toks, kb), bf16),) * (chips - 1),
        in_specs=[VM, VM],
        out_specs=(VM,) * chips,
        compiler_params=pltpu.CompilerParams(vmem_limit_bytes=2 << 20),
        cost_estimate=pl.CostEstimate(flops=chips * toks * kb, bytes_accessed=8 * chips * toks * kb, transcendentals=0),
    )(keep, got)


def chip_kernel(base, *refs):
    v = base[...]
    for r in refs[:-1]:
        v = v + r[...].astype(f32)
    refs[-1][...] = v.astype(refs[-1].dtype)


def chip_sum(base, parts, dtype):
    return pl.pallas_call(
        chip_kernel,
        out_shape=jax.ShapeDtypeStruct(base.shape, dtype),
        in_specs=[VM] * (1 + len(parts)),
        out_specs=VM,
        compiler_params=pltpu.CompilerParams(vmem_limit_bytes=2 << 20),
        cost_estimate=pl.CostEstimate(flops=base.size, bytes_accessed=8 * base.size, transcendentals=0),
    )(base, *parts)


def down_chunk_plain(block, h, back, wslot, wd, kb):
    experts, _, _ = h.shape
    blocks, toks, _ = back.shape
    w = lax.dynamic_slice_in_dim(wd, block * kb, kb, axis=2)
    v = jnp.einsum("erf,efd->erd", h, w, preferred_element_type=f32)
    v = (v * wslot).astype(bf16).reshape(experts, blocks, CAP, kb).swapaxes(0, 1).reshape(blocks, experts * CAP, kb)
    y = jnp.einsum("jts,jsd->jtd", back, v, preferred_element_type=f32).astype(bf16)
    y = y.reshape(blocks // 2, 2, toks, kb)
    return y[:, 0], y[:, 1]


def layer(tokens, routes, router_weight, gate_weight, up_weight, down_weight):
    experts = gate_weight.shape[0]
    blocks = lax.axis_size("expert")
    nh = lax.axis_size("hidden")
    chips = blocks // 2
    toks, kb = tokens.shape
    e_at = lax.axis_index("expert")
    h_at = lax.axis_index("hidden")
    kernels = kb % 128 == 0 and toks % 128 == 0

    def over_core(v):
        return lax.ppermute(v, "expert", [(i, i ^ 1) for i in range(blocks)])

    def over_x(v, d):
        return lax.ppermute(v, "expert", [(i, i ^ (2 * d)) for i in range(blocks)])

    def over_z(v, k):
        return lax.ppermute(v, "hidden", [(i, i ^ k) for i in range(nh)])

    def spread(v, held=None):
        evens = [v] + [over_x(v, d) for d in range(1, chips)]
        crossed = [over_core(w) for w in evens]
        if held is not None:
            evens[0] = held
        return [w for pair in zip(evens, crossed) for w in pair]

    names = spread(routes.T)
    slices = {0: tokens}
    top = nh - 1
    low = top ^ 1
    direct = [1, top] if nh >= 4 else list(range(1, nh))
    for k in direct:
        slices[k] = over_z(tokens, k)
    for k in range(2, nh - 1):
        if k == low and top in slices:
            slices[k] = over_z(slices[top], 1)
        else:
            slices[k] = over_z(tokens, k)
    order = [0] + direct + [k for k in range(2, nh - 1) if k not in direct]

    router = router_weight.T
    if kernels:
        gate_weight, up_weight, down_weight = (
            pltpu.with_memory_space_constraint(w, pltpu.HBM) for w in (gate_weight, up_weight, down_weight)
        )
        held, router, weights = first_fetch(h_at, tokens, router, gate_weight, up_weight)
    else:
        held = tokens

    planned = plan if kernels else plan_plain
    sel, back, sign = planned(e_at * experts, names, experts, router_weight.shape[1])

    down_order = [k for k in range(nh - 1, 0, -1)] + [0]
    acc = None
    small = []
    for at, k in enumerate(order):
        if kernels and at >= 2:
            slices[k], small[at - 2] = lax.optimization_barrier((slices[k], small[at - 2]))
        xs = spread(slices[k], held if k == 0 else None)
        last = at == nh - 1
        if kernels:
            after = h_at ^ (down_order[0] if last else order[at + 1])
            ahead = (down_weight,) if last else (gate_weight, up_weight)
            *acc, weights = up_chunk(h_at ^ k, after, xs, sel, sign, router, weights, ahead, acc, last)
            small.append(acc[-1])
        else:
            acc = up_chunk_plain(h_at ^ k, xs, sel, sign, router, gate_weight, up_weight, acc, last)
    h, wslot = acc

    total = []
    sent = []
    for at, k in enumerate(down_order):
        if kernels:
            after = None if at == nh - 1 else h_at ^ down_order[at + 1]
            gate = sent[at - 2] if at >= 2 else wslot
            keep, send, *more = down_chunk(after, h, back, wslot, weights, down_weight, gate)
            weights = more[0] if more else None
        else:
            keep, send = down_chunk_plain(h_at ^ k, h, back, wslot, down_weight, kb)
        got = over_core(send)
        if kernels:
            base, *outs = pair_sum(keep, got)
        else:
            both = keep.astype(f32) + got.astype(f32)
            base, outs = both[0], [both[d].astype(bf16) for d in range(1, chips)]
        sent.append(outs[-1] if outs else keep)
        parts = [over_x(v, d + 1) for d, v in enumerate(outs)]
        if k == 0:
            total = [base] + [v.astype(f32) for v in parts] + total
            continue
        if kernels:
            mid = chip_sum(base, parts, bf16)
        else:
            mid = sum([v.astype(f32) for v in parts], base).astype(bf16)
        total.append(over_z(mid, k).astype(f32))
    total = functools.reduce(jnp.add, total)
    return total.astype(bf16)


def solution(mesh):
    return jax.shard_map(
        layer,
        mesh=mesh,
        in_specs=(
            P(("groups", "expert"), "hidden"),
            P(("groups", "expert"), None),
            P(),
            P("expert", None, "hidden"),
            P("expert", None, "hidden"),
            P("expert", "hidden", None),
        ),
        out_specs=P(("groups", "expert"), "hidden"),
        check_vma=False,
    )
```

time: 210 us -> 92.1 us (0.44)
  waiting for transfers between devices: 90.1 us -> 25.6 us
  blocking collectives: 52.6 us -> 0 us
  Pallas kernels: 0 us -> 38.1 us
  matrix products: 35 us -> 0 us
  starting transfers between devices: 3.48 us -> 25.2 us
  between operations: 13.6 us -> 0.18 us
  local copies, waits for them, and re-layouts: 12.1 us -> 1.73 us
    reduce_scatter x1 -> x0, waiting for transfers between devices: 80.6 us -> none  [per_device(): lax.psum_scatter(partial_value, 'hidden', scatter_dimension=2, tiled=True)]
    pallas_call x0 -> x17, Pallas kernels: none -> 38.1 us  [the longest x4 21.5 us: up_chunk(): pl.pallas_call(functools.partial(up_kernel, first, last, blocks, experts)...]
    dot_general x4 -> x0, matrix products: 35 us -> none  [the longest x1 12.9 us: per_device(): jnp.einsum('erf,efd->erd', hidden_act, down_weight, preferred_element_typ...]
    all_to_all x1 -> x0, blocking collectives: 31 us -> none  [per_device(): lax.all_to_all(send_rows, 'expert', split_axis=0, concat_axis=1, tiled=True)]
    ppermute x0 -> x29, waiting for transfers between devices: none -> 25.6 us  [the longest x9 16.1 us: over_x(): return lax.ppermute(v, 'expert', [(i, i ^ 2 * d) for i in range(blocks)])]
    ppermute x0 -> x29, starting transfers between devices: none -> 25.2 us  [the longest x9 11.5 us: over_x(): return lax.ppermute(v, 'expert', [(i, i ^ 2 * d) for i in range(blocks)])]
    all_gather x1 -> x0, blocking collectives: 21.5 us -> none  [per_device(): gathered = lax.all_gather(tokens, 'hidden', axis=1, tiled=True)]
    all_to_all x1 -> x0, waiting for transfers between devices: 9.45 us -> none  [per_device(): lax.all_to_all(summed, 'expert', split_axis=1, concat_axis=0, tiled=True)]
  transfers between devices with their start and end apart: 2 -> 29, of which waited for: 2 -> 6; matrix products, arithmetic and copies ran while one was open for 1% -> 0% of each run, Pallas kernels for 0% -> 33%
where the time goes in v1:
time: 92.1 us; the launch traced here: 92 us
  Pallas kernels  38.1 us (41%)
  waiting for transfers between devices  25.6 us (28%)
  starting transfers between devices  25.2 us (27%)
  local copies, waits for them, and re-layouts  1.73 us (2%)
  other arithmetic  1.09 us (1%)
    pallas_call x4, Pallas kernels, up_chunk(): pl.pallas_call(functools.partial(up_kernel, first, last, blocks, experts)...  21.5 us
    ppermute x9, waiting for transfers between devices, over_x(): return lax.ppermute(v, 'expert', [(i, i ^ 2 * d) for i in range(blocks)])  16.1 us
    ppermute x9, starting transfers between devices, over_x(): return lax.ppermute(v, 'expert', [(i, i ^ 2 * d) for i in range(blocks)])  11.5 us
    pallas_call x4, Pallas kernels, down_chunk(): pl.pallas_call(functools.partial(down_kernel, experts, blocks, last), out...  10.6 us
    ppermute x6, starting transfers between devices, over_z(): return lax.ppermute(v, 'hidden', [(i, i ^ k) for i in range(nh)])  10.5 us
    ppermute x6, waiting for transfers between devices, over_z(): return lax.ppermute(v, 'hidden', [(i, i ^ k) for i in range(nh)])  9.5 us
    pallas_call x1, Pallas kernels, first_fetch(): pl.pallas_call(first_kernel, out_shape=(jax.ShapeDtypeStruct(tokens.shape...  4.99 us
    ppermute x14, starting transfers between devices, over_core(): return lax.ppermute(v, 'expert', [(i, i ^ 1) for i in range(blocks)])  3.18 us
  transfers between devices with their start and end apart: 29, of which 6 were waited for; matrix products, arithmetic and copies ran while one was open for 0% of the time, Pallas kernels for 33%

profile of v1, /device:TPU:0, one launch (start us, length us, event | category | flops | bytes accessed | tf_op | source)
XLA Modules:
  0.0 92.0 jit_solution(14854401282517989778)
XLA Ops:
  0.0 3.0 %collective-permute-start.10 = (bf16[128,768]{1,0:T(8,128)(2,1)}, bf16[128,768]{1,0:T(8,128)(2,1)S(1)}, u32[]{:S(2)}, u32[]{:S(2)}) collective-permute-start(bf16[128,768]{1,0:T(8,128)(2,1)} %tokens.1), channel_id=1, source_target_pairs={{0,8},{4,12},{8,0},{12,4},{1,9},{5,13},{9,1},{13,5},{2,10},{6,14},... | collective-permute-start | bytes 589832 | tf_op jit(solution)/shard_map/ppermute | solution.py:358
  3.0 1.6 %collective-permute-start.2 = (bf16[128,768]{1,0:T(8,128)(2,1)}, bf16[128,768]{1,0:T(8,128)(2,1)S(1)}, u32[]{:S(2)}, u32[]{:S(2)}) collective-permute-start(bf16[128,768]{1,0:T(8,128)(2,1)} %tokens.1), channel_id=1, source_target_pairs={{0,1},{1,0},{2,3},{3,2},{4,5},{5,4},{6,7},{7,6},{8,9},{9,8},{10,11... | collective-permute-start | bytes 589832 | tf_op jit(solution)/shard_map/ppermute | solution.py:361
  4.5 0.5 collective-permute-start.7
  5.6 2.7 %collective-permute-done.7.refs_2_ = s32[2,128]{1,0:T(2,128)S(1)} collective-permute-done((s32[2,128]{1,0:T(2,128)}, s32[2,128]{1,0:T(2,128)S(1)}, u32[]{:S(2)}, u32[]{:S(2)}) %collective-permute-start.7) | collective-permute-done | bytes 1056 | tf_op jit(solution)/shard_map/ppermute | solution.py:358
  8.3 3.7 %collective-permute-start = (bf16[128,768]{1,0:T(8,128)(2,1)}, bf16[128,768]{1,0:T(8,128)(2,1)S(1)}, u32[]{:S(2)}, u32[]{:S(2)}) collective-permute-start(bf16[128,768]{1,0:T(8,128)(2,1)} %tokens.1), channel_id=1, source_target_pairs={{0,3},{1,2},{2,1},{3,0},{4,7},{5,6},{6,5},{7,4},{8,11},{9,10},{10,... | collective-permute-start | bytes 589832 | tf_op jit(solution)/shard_map/ppermute | solution.py:361
  12.0 1.6 %collective-permute-start.4 = (bf16[128,768]{1,0:T(8,128)(2,1)S(1)}, bf16[128,768]{1,0:T(8,128)(2,1)S(1)}, u32[]{:S(2)}, u32[]{:S(2)}) collective-permute-start(bf16[128,768]{1,0:T(8,128)(2,1)S(1)} %collective-permute-done.2.refs_1_), channel_id=1, source_target_pairs={{0,8},{4,12},{8,0},{12,4},{1,9},{5,13},{9,1},{13,5},{2,10},{6,14},... | collective-permute-start | bytes 589832 | tf_op jit(solution)/shard_map/ppermute | solution.py:358
  13.9 0.9 %copy-done = bf16[128,768]{1,0:T(8,128)(2,1)S(1)} copy-done((bf16[128,768]{1,0:T(8,128)(2,1)S(1)}, bf16[128,768]{1,0:T(8,128)(2,1)}, u32[]{:S(2)}) %copy-start) | copy-done | bytes 196632
  14.8 0.8 copy-done.1
  15.6 5.0 %shard_map.65 = (bf16[128,768]{1,0:T(8,128)(2,1)S(1)}, bf16[8,3072]{1,0:T(8,128)(2,1)S(1)}, bf16[2,2,768,2048]{3,2,1,0:T(8,128)(2,1)S(1)}) custom-call(s32[1]{0:T(128)} %bitcast.5.idx.refs_0_, bf16[128,768]{1,0:T(8,128)(2,1)S(1)} %copy-done, bf16[8,3072]{1,0:T(8,128)(2,1)S(1)} %bitcast.7, bf16[2,3072,2048]{2,1,0:T(8,128)(2,1)} %refs_8_.6, ...), custom_call_target="tpu_custom_call" | custom-call | bytes 12582912 | tf_op jit(solution)/shard_map/pallas_call | solution.py:114
  21.8 5.3 %shard_map.66 = (f32[2,192,2048]{2,1,0:T(8,128)S(1)}, f32[2,192,2048]{2,1,0:T(8,128)S(1)}, f32[4,8,128]{2,1,0:T(8,128)S(1)}, bf16[2,2,768,2048]{3,2,1,0:T(8,128)(2,1)S(1)}) custom-call(s32[2]{0:T(128)S(1)} %pad_add_fusion.2.refs_0_, bf16[128,768]{1,0:T(8,128)(2,1)S(1)} %get-tuple-element.49.refs_1_, bf16[128,768]{1,0:T(8,128)(2,1)S(1)} %collective-permute-done.9.refs_2_, ...), custom_call_target="tpu_custom_call" | custom-call | flops 2415919104 | bytes 12582912 | tf_op jit(solution)/shard_map/pallas_call | solution.py:208
  27.1 0.6 collective-permute-start.16
  27.8 5.5 %shard_map.67 = (f32[2,192,2048]{2,1,0:T(8,128)S(1)}, f32[2,192,2048]{2,1,0:T(8,128)S(1)}, f32[4,8,128]{2,1,0:T(8,128)S(1)}, bf16[2,2,768,2048]{3,2,1,0:T(8,128)(2,1)S(1)}) custom-call(s32[2]{0:T(128)S(1)} %pad_add_fusion.1.refs_0_, ...), custom_call_target="tpu_custom_call", output_to_operand_aliasing={{0}: (10, {}), {1}: (11, {}), {2}: (12, {})} | custom-call | flops 2415919104 | bytes 12582912 | tf_op jit(solution)/shard_map/pallas_call | solution.py:208
  33.3 1.6 %collective-permute-start.13 = (bf16[128,768]{1,0:T(8,128)(2,1)S(1)}, bf16[128,768]{1,0:T(8,128)(2,1)S(1)}, u32[]{:S(2)}, u32[]{:S(2)}) collective-permute-start(bf16[128,768]{1,0:T(8,128)(2,1)S(1)} %collective-permute-done.1.refs_1_), channel_id=1, source_target_pairs={{0,8},{4,12},{8,0},{12,4},{1,9},{5,13},{9,1},{13,5},{2,10},{6,14},... | collective-permute-start | bytes 589832 | tf_op jit(solution)/shard_map/ppermute | solution.py:358
  35.5 5.1 %collective-permute-done.13.refs_3_ = bf16[128,768]{1,0:T(8,128)(2,1)S(1)} collective-permute-done((bf16[128,768]{1,0:T(8,128)(2,1)S(1)}, bf16[128,768]{1,0:T(8,128)(2,1)S(1)}, u32[]{:S(2)}, u32[]{:S(2)}) %collective-permute-start.13) | collective-permute-done | bytes 196640 | tf_op jit(solution)/shard_map/ppermute | solution.py:358
  40.6 5.5 %shard_map.68 = (f32[2,192,2048]{2,1,0:T(8,128)S(1)}, f32[2,192,2048]{2,1,0:T(8,128)S(1)}, f32[4,8,128]{2,1,0:T(8,128)S(1)}, bf16[2,2,768,2048]{3,2,1,0:T(8,128)(2,1)S(1)}) custom-call(s32[2]{0:T(128)S(1)} %pad_add_fusion.3.refs_0_, bf16[128,768]{1,0:T(8,128)(2,1)S(1)} %collective-permute-done.refs_1_, ...), custom_call_target="tpu_custom_call", output_to_operand_aliasing={{0}: (10, {}), {1}: (11, {}), {2}: (12, {})} | custom-call | flops 2415919104 | bytes 12582912 | tf_op jit(solution)/shard_map/pallas_call | solution.py:208
  46.1 5.3 %shard_map.69 = (bf16[2,192,2048]{2,1,0:T(8,128)(2,1)S(1)}, f32[2,192,1]{2,1,0:T(8,128)S(1)}, bf16[2,2048,768]{2,1,0:T(8,128)(2,1)S(1)}) custom-call(s32[2]{0:T(128)S(1)} %pad_add_fusion.refs_0_, bf16[128,768]{1,0:T(8,128)(2,1)S(1)} %collective-permute-done.1.refs_1_, bf16[128,768]{1,0:T(8,128)(2,1)S(1)} %collective-permute-done.12.refs_2_, ...), custom_call_target="tpu_custom_call" | custom-call | flops 2415919104 | bytes 12582912 | tf_op jit(solution)/shard_map/pallas_call | solution.py:208
  51.4 2.9 %shard_map.70 = (bf16[2,128,768]{2,1,0:T(8,128)(2,1)S(1)}, bf16[2,128,768]{2,1,0:T(8,128)(2,1)S(1)}, bf16[2,2048,768]{2,1,0:T(8,128)(2,1)S(1)}) custom-call(s32[1]{0:T(128)} %bitcast.refs_0_, bf16[2,192,2048]{2,1,0:T(8,128)(2,1)S(1)} %get-tuple-element.66.refs_1_, bf16[4,128,96]{2,1,0:T(8,128)(2,1)S(1)} %get-tuple-element.67.refs_2_, ...), custom_call_target="tpu_custom_call" | custom-call | flops 1207959552 | bytes 6291456 | tf_op jit(solution)/shard_map/pallas_call | solution.py:280
  54.3 0.5 collective-permute-start.18
  54.8 2.9 %shard_map.71 = (bf16[2,128,768]{2,1,0:T(8,128)(2,1)S(1)}, bf16[2,128,768]{2,1,0:T(8,128)(2,1)S(1)}, bf16[2,2048,768]{2,1,0:T(8,128)(2,1)S(1)}) custom-call(s32[1]{0:T(128)} %bitcast.2.refs_0_, bf16[2,192,2048]{2,1,0:T(8,128)(2,1)S(1)} %get-tuple-element.66.refs_1_, bf16[4,128,96]{2,1,0:T(8,128)(2,1)S(1)} %get-tuple-element.67.refs_2_, ...), custom_call_target="tpu_custom_call" | custom-call | flops 1207959552 | bytes 6291456 | tf_op jit(solution)/shard_map/pallas_call | solution.py:280
  57.9 2.9 %shard_map.73 = (bf16[2,128,768]{2,1,0:T(8,128)(2,1)S(1)}, bf16[2,128,768]{2,1,0:T(8,128)(2,1)S(1)}, bf16[2,2048,768]{2,1,0:T(8,128)(2,1)S(1)}) custom-call(s32[1]{0:T(128)} %bitcast.5.idx.refs_0_, bf16[2,192,2048]{2,1,0:T(8,128)(2,1)S(1)} %get-tuple-element.66.refs_1_, bf16[4,128,96]{2,1,0:T(8,128)(2,1)S(1)} %get-tuple-element.67.refs_2_, ...), custom_call_target="tpu_custom_call" | custom-call | flops 1207959552 | bytes 6291456 | tf_op jit(solution)/shard_map/pallas_call | solution.py:280
  61.5 1.9 %shard_map.75 = (bf16[2,128,768]{2,1,0:T(8,128)(2,1)S(1)}, bf16[2,128,768]{2,1,0:T(8,128)(2,1)S(1)}) custom-call(s32[1]{0:T(128)} %constant.3.clone.1.refs_0_, bf16[2,192,2048]{2,1,0:T(8,128)(2,1)S(1)} %get-tuple-element.66.refs_1_, bf16[4,128,96]{2,1,0:T(8,128)(2,1)S(1)} %get-tuple-element.67.refs_2_, f32[2,192,1]{2,1,0:T(8,128)S(1)} %get-tuple-element.68.refs_3_.refs_5_, ...), custom_call_target="tpu_custom_call" | custom-call | flops 1207959552 | bytes 6291456 | tf_op jit(solution)/shard_map/pallas_call | solution.py:280
  63.5 1.5 %collective-permute-start.22 = (bf16[128,768]{1,0:T(8,128)(2,1)S(1)}, bf16[128,768]{1,0:T(8,128)(2,1)S(1)}, u32[]{:S(2)}, u32[]{:S(2)}) collective-permute-start(bf16[128,768]{1,0:T(8,128)(2,1)S(1)} %get-tuple-element.74.refs_5_), channel_id=1, source_target_pairs={{0,8},{4,12},{8,0},{12,4},{1,9},{5,13},{9,1},{13,5},{2,10},{6,14},... | collective-permute-start | bytes 589832 | tf_op jit(solution)/shard_map/ppermute | solution.py:358
  65.7 1.6 %collective-permute-start.27 = (bf16[128,768]{1,0:T(8,128)(2,1)S(1)}, bf16[128,768]{1,0:T(8,128)(2,1)S(1)}, u32[]{:S(2)}, u32[]{:S(2)}) collective-permute-start(bf16[128,768]{1,0:T(8,128)(2,1)S(1)} %get-tuple-element.88), channel_id=1, source_target_pairs={{0,8},{4,12},{8,0},{12,4},{1,9},{5,13},{9,1},{13,5},{2,10},{6,14},... | collective-permute-start | bytes 589832 | tf_op jit(solution)/shard_map/ppermute | solution.py:358
  67.3 4.1 %collective-permute-done.22.refs_0_ = bf16[128,768]{1,0:T(8,128)(2,1)S(1)} collective-permute-done((bf16[128,768]{1,0:T(8,128)(2,1)S(1)}, bf16[128,768]{1,0:T(8,128)(2,1)S(1)}, u32[]{:S(2)}, u32[]{:S(2)}) %collective-permute-start.22) | collective-permute-done | bytes 196640 | tf_op jit(solution)/shard_map/ppermute | solution.py:358
  71.4 1.9 %collective-permute-start.23 = (bf16[128,768]{1,0:T(8,128)(2,1)S(1)}, bf16[128,768]{1,0:T(8,128)(2,1)S(1)}, u32[]{:S(2)}, u32[]{:S(2)}) collective-permute-start(bf16[128,768]{1,0:T(8,128)(2,1)S(1)} %shard_map.77), channel_id=1, source_target_pairs={{0,3},{1,2},{2,1},{3,0},{4,7},{5,6},{6,5},{7,4},{8,11},{9,10},{10,... | collective-permute-start | bytes 589832 | tf_op jit(solution)/shard_map/ppermute | solution.py:361
  73.2 2.3 %collective-permute-done.24.refs_0_ = bf16[128,768]{1,0:T(8,128)(2,1)S(1)} collective-permute-done((bf16[128,768]{1,0:T(8,128)(2,1)S(1)}, bf16[128,768]{1,0:T(8,128)(2,1)S(1)}, u32[]{:S(2)}, u32[]{:S(2)}) %collective-permute-start.24) | collective-permute-done | bytes 196640 | tf_op jit(solution)/shard_map/ppermute | solution.py:358
  75.6 1.5 %collective-permute-start.25 = (bf16[128,768]{1,0:T(8,128)(2,1)S(1)}, bf16[128,768]{1,0:T(8,128)(2,1)S(1)}, u32[]{:S(2)}, u32[]{:S(2)}) collective-permute-start(bf16[128,768]{1,0:T(8,128)(2,1)S(1)} %shard_map.78), channel_id=1, source_target_pairs={{0,2},{1,3},{2,0},{3,1},{4,6},{5,7},{6,4},{7,5},{8,10},{9,11},{10,... | collective-permute-start | bytes 589832 | tf_op jit(solution)/shard_map/ppermute | solution.py:361
  77.2 0.7 collective-permute-start.21
  77.9 1.9 %collective-permute-done.27.refs_0_ = bf16[128,768]{1,0:T(8,128)(2,1)S(1)} collective-permute-done((bf16[128,768]{1,0:T(8,128)(2,1)S(1)}, bf16[128,768]{1,0:T(8,128)(2,1)S(1)}, u32[]{:S(2)}, u32[]{:S(2)}) %collective-permute-start.27) | collective-permute-done | bytes 196640 | tf_op jit(solution)/shard_map/ppermute | solution.py:358
  79.8 1.9 %collective-permute-start.28 = (bf16[128,768]{1,0:T(8,128)(2,1)S(1)}, bf16[128,768]{1,0:T(8,128)(2,1)S(1)}, u32[]{:S(2)}, u32[]{:S(2)}) collective-permute-start(bf16[128,768]{1,0:T(8,128)(2,1)S(1)} %shard_map.80), channel_id=1, source_target_pairs={{0,1},{1,0},{2,3},{3,2},{4,5},{5,4},{6,7},{7,6},{8,9},{9,8},{10,11... | collective-permute-start | bytes 589832 | tf_op jit(solution)/shard_map/ppermute | solution.py:361
  81.7 9.5 %collective-permute-done.25 = bf16[128,768]{1,0:T(8,128)(2,1)S(1)} collective-permute-done((bf16[128,768]{1,0:T(8,128)(2,1)S(1)}, bf16[128,768]{1,0:T(8,128)(2,1)S(1)}, u32[]{:S(2)}, u32[]{:S(2)}) %collective-permute-start.25) | collective-permute-done | bytes 196640 | tf_op jit(solution)/shard_map/ppermute | solution.py:361
  91.2 0.8 add_convert_fusion
  (54 shorter events, 4.5 us)
Async XLA Ops:
  0.0 12.0 %collective-permute-start.10 = (bf16[128,768]{1,0:T(8,128)(2,1)}, bf16[128,768]{1,0:T(8,128)(2,1)S(1)}, u32[]{:S(2)}, u32[]{:S(2)}) collective-permute-start(bf16[128,768]{1,0:T(8,128)(2,1)} %tokens.1), channel_id=1, source_target_pairs={{0,8},{4,12},{8,0},{12,4},{1,9},{5,13},{9,1},{13,5},{2,10},{6,14},... | collective-permute-start | bytes 589832 | tf_op jit(solution)/shard_map/ppermute | solution.py:358
  3.0 9.0 %collective-permute-start.2 = (bf16[128,768]{1,0:T(8,128)(2,1)}, bf16[128,768]{1,0:T(8,128)(2,1)S(1)}, u32[]{:S(2)}, u32[]{:S(2)}) collective-permute-start(bf16[128,768]{1,0:T(8,128)(2,1)} %tokens.1), channel_id=1, source_target_pairs={{0,1},{1,0},{2,3},{3,2},{4,5},{5,4},{6,7},{7,6},{8,9},{9,8},{10,11... | collective-permute-start | bytes 589832 | tf_op jit(solution)/shard_map/ppermute | solution.py:361
  4.5 3.8 %collective-permute-start.7 = (s32[2,128]{1,0:T(2,128)}, s32[2,128]{1,0:T(2,128)S(1)}, u32[]{:S(2)}, u32[]{:S(2)}) collective-permute-start(s32[2,128]{1,0:T(2,128)} %bitcast.8), channel_id=1, source_target_pairs={{0,8},{4,12},{8,0},{12,4},{1,9},{5,13},{9,1},{13,5},{2,10},{6,14},... | collective-permute-start | bytes 3080 | tf_op jit(solution)/shard_map/ppermute | solution.py:358
  5.1 8.6 %collective-permute-start.6 = (s32[2,128]{1,0:T(2,128)}, s32[2,128]{1,0:T(2,128)S(1)}, u32[]{:S(2)}, u32[]{:S(2)}) collective-permute-start(s32[2,128]{1,0:T(2,128)} %bitcast.9), channel_id=1, source_target_pairs={{0,4},{4,0},{8,12},{12,8},{1,5},{5,1},{9,13},{13,9},{2,6},{6,2},{1... | collective-permute-start | bytes 3080 | tf_op jit(solution)/shard_map/ppermute | solution.py:355
  5.1 16.7 %collective-permute-start.9 = (bf16[128,768]{1,0:T(8,128)(2,1)}, bf16[128,768]{1,0:T(8,128)(2,1)S(1)}, u32[]{:S(2)}, u32[]{:S(2)}) collective-permute-start(bf16[128,768]{1,0:T(8,128)(2,1)} %tokens.1), channel_id=1, source_target_pairs={{0,4},{4,0},{8,12},{12,8},{1,5},{5,1},{9,13},{13,9},{2,6},{6,2},{1... | collective-permute-start | bytes 589832 | tf_op jit(solution)/shard_map/ppermute | solution.py:355
  8.3 13.2 %collective-permute-start = (bf16[128,768]{1,0:T(8,128)(2,1)}, bf16[128,768]{1,0:T(8,128)(2,1)S(1)}, u32[]{:S(2)}, u32[]{:S(2)}) collective-permute-start(bf16[128,768]{1,0:T(8,128)(2,1)} %tokens.1), channel_id=1, source_target_pairs={{0,3},{1,2},{2,1},{3,0},{4,7},{5,6},{6,5},{7,4},{8,11},{9,10},{10,... | collective-permute-start | bytes 589832 | tf_op jit(solution)/shard_map/ppermute | solution.py:361
  12.0 9.8 %collective-permute-start.11 = (bf16[128,768]{1,0:T(8,128)(2,1)S(1)}, bf16[128,768]{1,0:T(8,128)(2,1)S(1)}, u32[]{:S(2)}, u32[]{:S(2)}) collective-permute-start(bf16[128,768]{1,0:T(8,128)(2,1)S(1)} %collective-permute-done.10.refs_3_), channel_id=1, source_target_pairs={{0,4},{4,0},{8,12},{12,8},{1,5},{5,1},{9,13},{13,9},{2,6},{6,2},{1... | collective-permute-start | bytes 589832 | tf_op jit(solution)/shard_map/ppermute | solution.py:355
  12.0 9.6 %collective-permute-start.4 = (bf16[128,768]{1,0:T(8,128)(2,1)S(1)}, bf16[128,768]{1,0:T(8,128)(2,1)S(1)}, u32[]{:S(2)}, u32[]{:S(2)}) collective-permute-start(bf16[128,768]{1,0:T(8,128)(2,1)S(1)} %collective-permute-done.2.refs_1_), channel_id=1, source_target_pairs={{0,8},{4,12},{8,0},{12,4},{1,9},{5,13},{9,1},{13,5},{2,10},{6,14},... | collective-permute-start | bytes 589832 | tf_op jit(solution)/shard_map/ppermute | solution.py:358
  13.6 7.0 %collective-permute-start.8 = (s32[2,128]{1,0:T(2,128)S(1)}, s32[2,128]{1,0:T(2,128)S(1)}, u32[]{:S(2)}, u32[]{:S(2)}) collective-permute-start(s32[2,128]{1,0:T(2,128)S(1)} %collective-permute-done.7.refs_2_), channel_id=1, source_target_pairs={{0,4},{4,0},{8,12},{12,8},{1,5},{5,1},{9,13},{13,9},{2,6},{6,2},{1... | collective-permute-start | bytes 3080 | tf_op jit(solution)/shard_map/ppermute | solution.py:355
  13.9 0.9 %copy-start = (bf16[128,768]{1,0:T(8,128)(2,1)S(1)}, bf16[128,768]{1,0:T(8,128)(2,1)}, u32[]{:S(2)}) copy-start(bf16[128,768]{1,0:T(8,128)(2,1)} %tokens.1) | copy-start | bytes 589828
  14.8 0.8 copy-start.1
  15.6 5.0 %copy-start.2 = (s32[128,2]{0,1:T(2,128)S(1)}, s32[128,2]{0,1:T(2,128)}, u32[]{:S(2)}) copy-start(s32[128,2]{0,1:T(2,128)} %param.7) | copy-start | bytes 3076
  21.1 6.6 %collective-permute-start.3 = (bf16[128,768]{1,0:T(8,128)(2,1)S(1)}, bf16[128,768]{1,0:T(8,128)(2,1)S(1)}, u32[]{:S(2)}, u32[]{:S(2)}) collective-permute-start(bf16[128,768]{1,0:T(8,128)(2,1)S(1)} %collective-permute-done.2.refs_1_), channel_id=1, source_target_pairs={{0,4},{4,0},{8,12},{12,8},{1,5},{5,1},{9,13},{13,9},{2,6},{6,2},{1... | collective-permute-start | bytes 589832 | tf_op jit(solution)/shard_map/ppermute | solution.py:355
  21.6 11.7 %collective-permute-start.1 = (bf16[128,768]{1,0:T(8,128)(2,1)S(1)}, bf16[128,768]{1,0:T(8,128)(2,1)S(1)}, u32[]{:S(2)}, u32[]{:S(2)}) collective-permute-start(bf16[128,768]{1,0:T(8,128)(2,1)S(1)} %collective-permute-done.refs_1_), channel_id=1, source_target_pairs={{0,1},{1,0},{2,3},{3,2},{4,5},{5,4},{6,7},{7,6},{8,9},{9,8},{10,11... | collective-permute-start | bytes 589832 | tf_op jit(solution)/shard_map/ppermute | solution.py:361
  21.6 6.2 %collective-permute-start.5 = (bf16[128,768]{1,0:T(8,128)(2,1)S(1)}, bf16[128,768]{1,0:T(8,128)(2,1)S(1)}, u32[]{:S(2)}, u32[]{:S(2)}) collective-permute-start(bf16[128,768]{1,0:T(8,128)(2,1)S(1)} %collective-permute-done.4.refs_3_), channel_id=1, source_target_pairs={{0,4},{4,0},{8,12},{12,8},{1,5},{5,1},{9,13},{13,9},{2,6},{6,2},{1... | collective-permute-start | bytes 589832 | tf_op jit(solution)/shard_map/ppermute | solution.py:355
  27.1 7.7 %collective-permute-start.16 = (bf16[128,768]{1,0:T(8,128)(2,1)S(1)}, bf16[128,768]{1,0:T(8,128)(2,1)S(1)}, u32[]{:S(2)}, u32[]{:S(2)}) collective-permute-start(bf16[128,768]{1,0:T(8,128)(2,1)S(1)} %collective-permute-done.refs_1_), channel_id=1, source_target_pairs={{0,8},{4,12},{8,0},{12,4},{1,9},{5,13},{9,1},{13,5},{2,10},{6,14},... | collective-permute-start | bytes 589832 | tf_op jit(solution)/shard_map/ppermute | solution.py:358
  27.7 12.9 %collective-permute-start.15 = (bf16[128,768]{1,0:T(8,128)(2,1)S(1)}, bf16[128,768]{1,0:T(8,128)(2,1)S(1)}, u32[]{:S(2)}, u32[]{:S(2)}) collective-permute-start(bf16[128,768]{1,0:T(8,128)(2,1)S(1)} %collective-permute-done.refs_1_), channel_id=1, source_target_pairs={{0,4},{4,0},{8,12},{12,8},{1,5},{5,1},{9,13},{13,9},{2,6},{6,2},{1... | collective-permute-start | bytes 589832 | tf_op jit(solution)/shard_map/ppermute | solution.py:355
  33.3 7.3 %collective-permute-start.13 = (bf16[128,768]{1,0:T(8,128)(2,1)S(1)}, bf16[128,768]{1,0:T(8,128)(2,1)S(1)}, u32[]{:S(2)}, u32[]{:S(2)}) collective-permute-start(bf16[128,768]{1,0:T(8,128)(2,1)S(1)} %collective-permute-done.1.refs_1_), channel_id=1, source_target_pairs={{0,8},{4,12},{8,0},{12,4},{1,9},{5,13},{9,1},{13,5},{2,10},{6,14},... | collective-permute-start | bytes 589832 | tf_op jit(solution)/shard_map/ppermute | solution.py:358
  34.8 5.8 %collective-permute-start.17 = (bf16[128,768]{1,0:T(8,128)(2,1)S(1)}, bf16[128,768]{1,0:T(8,128)(2,1)S(1)}, u32[]{:S(2)}, u32[]{:S(2)}) collective-permute-start(bf16[128,768]{1,0:T(8,128)(2,1)S(1)} %collective-permute-done.16.refs_3_), channel_id=1, source_target_pairs={{0,4},{4,0},{8,12},{12,8},{1,5},{5,1},{9,13},{13,9},{2,6},{6,2},{1... | collective-permute-start | bytes 589832 | tf_op jit(solution)/shard_map/ppermute | solution.py:355
  35.1 10.9 %collective-permute-start.12 = (bf16[128,768]{1,0:T(8,128)(2,1)S(1)}, bf16[128,768]{1,0:T(8,128)(2,1)S(1)}, u32[]{:S(2)}, u32[]{:S(2)}) collective-permute-start(bf16[128,768]{1,0:T(8,128)(2,1)S(1)} %collective-permute-done.1.refs_1_), channel_id=1, source_target_pairs={{0,4},{4,0},{8,12},{12,8},{1,5},{5,1},{9,13},{13,9},{2,6},{6,2},{1... | collective-permute-start | bytes 589832 | tf_op jit(solution)/shard_map/ppermute | solution.py:355
  40.6 5.5 %collective-permute-start.14 = (bf16[128,768]{1,0:T(8,128)(2,1)S(1)}, bf16[128,768]{1,0:T(8,128)(2,1)S(1)}, u32[]{:S(2)}, u32[]{:S(2)}) collective-permute-start(bf16[128,768]{1,0:T(8,128)(2,1)S(1)} %collective-permute-done.13.refs_3_), channel_id=1, source_target_pairs={{0,4},{4,0},{8,12},{12,8},{1,5},{5,1},{9,13},{13,9},{2,6},{6,2},{1... | collective-permute-start | bytes 589832 | tf_op jit(solution)/shard_map/ppermute | solution.py:355
  54.3 3.5 %collective-permute-start.18 = (bf16[2,128,768]{2,1,0:T(8,128)(2,1)S(1)}, bf16[2,128,768]{2,1,0:T(8,128)(2,1)S(1)}, u32[]{:S(2)}, u32[]{:S(2)}) collective-permute-start(bf16[2,128,768]{2,1,0:T(8,128)(2,1)S(1)} %get-tuple-element.73), channel_id=1, source_target_pairs={{0,4},{4,0},{8,12},{12,8},{1,5},{5,1},{9,13},{13,9},{2,6},{6,2},{1... | collective-permute-start | bytes 1179656 | tf_op jit(solution)/shard_map/ppermute | solution.py:355
  57.7 3.6 %collective-permute-start.19 = (bf16[2,128,768]{2,1,0:T(8,128)(2,1)S(1)}, bf16[2,128,768]{2,1,0:T(8,128)(2,1)S(1)}, u32[]{:S(2)}, u32[]{:S(2)}) collective-permute-start(bf16[2,128,768]{2,1,0:T(8,128)(2,1)S(1)} %get-tuple-element.77), channel_id=1, source_target_pairs={{0,4},{4,0},{8,12},{12,8},{1,5},{5,1},{9,13},{13,9},{2,6},{6,2},{1... | collective-permute-start | bytes 1179656 | tf_op jit(solution)/shard_map/ppermute | solution.py:355
  60.8 4.8 %collective-permute-start.26 = (bf16[2,128,768]{2,1,0:T(8,128)(2,1)S(1)}, bf16[2,128,768]{2,1,0:T(8,128)(2,1)S(1)}, u32[]{:S(2)}, u32[]{:S(2)}) collective-permute-start(bf16[2,128,768]{2,1,0:T(8,128)(2,1)S(1)} %get-tuple-element.86), channel_id=1, source_target_pairs={{0,4},{4,0},{8,12},{12,8},{1,5},{5,1},{9,13},{13,9},{2,6},{6,2},{1... | collective-permute-start | bytes 1179656 | tf_op jit(solution)/shard_map/ppermute | solution.py:355
  63.4 13.7 %collective-permute-start.20 = (bf16[2,128,768]{2,1,0:T(8,128)(2,1)S(1)}, bf16[2,128,768]{2,1,0:T(8,128)(2,1)S(1)}, u32[]{:S(2)}, u32[]{:S(2)}) collective-permute-start(bf16[2,128,768]{2,1,0:T(8,128)(2,1)S(1)} %get-tuple-element.80), channel_id=1, source_target_pairs={{0,4},{4,0},{8,12},{12,8},{1,5},{5,1},{9,13},{13,9},{2,6},{6,2},{1... | collective-permute-start | bytes 1179656 | tf_op jit(solution)/shard_map/ppermute | solution.py:355
  63.5 7.8 %collective-permute-start.22 = (bf16[128,768]{1,0:T(8,128)(2,1)S(1)}, bf16[128,768]{1,0:T(8,128)(2,1)S(1)}, u32[]{:S(2)}, u32[]{:S(2)}) collective-permute-start(bf16[128,768]{1,0:T(8,128)(2,1)S(1)} %get-tuple-element.74.refs_5_), channel_id=1, source_target_pairs={{0,8},{4,12},{8,0},{12,4},{1,9},{5,13},{9,1},{13,5},{2,10},{6,14},... | collective-permute-start | bytes 589832 | tf_op jit(solution)/shard_map/ppermute | solution.py:358
  65.0 10.5 %collective-permute-start.24 = (bf16[128,768]{1,0:T(8,128)(2,1)S(1)}, bf16[128,768]{1,0:T(8,128)(2,1)S(1)}, u32[]{:S(2)}, u32[]{:S(2)}) collective-permute-start(bf16[128,768]{1,0:T(8,128)(2,1)S(1)} %get-tuple-element.78.refs_5_), channel_id=1, source_target_pairs={{0,8},{4,12},{8,0},{12,4},{1,9},{5,13},{9,1},{13,5},{2,10},{6,14},... | collective-permute-start | bytes 589832 | tf_op jit(solution)/shard_map/ppermute | solution.py:358
  65.7 14.1 %collective-permute-start.27 = (bf16[128,768]{1,0:T(8,128)(2,1)S(1)}, bf16[128,768]{1,0:T(8,128)(2,1)S(1)}, u32[]{:S(2)}, u32[]{:S(2)}) collective-permute-start(bf16[128,768]{1,0:T(8,128)(2,1)S(1)} %get-tuple-element.88), channel_id=1, source_target_pairs={{0,8},{4,12},{8,0},{12,4},{1,9},{5,13},{9,1},{13,5},{2,10},{6,14},... | collective-permute-start | bytes 589832 | tf_op jit(solution)/shard_map/ppermute | solution.py:358
  71.4 10.3 %collective-permute-start.23 = (bf16[128,768]{1,0:T(8,128)(2,1)S(1)}, bf16[128,768]{1,0:T(8,128)(2,1)S(1)}, u32[]{:S(2)}, u32[]{:S(2)}) collective-permute-start(bf16[128,768]{1,0:T(8,128)(2,1)S(1)} %shard_map.77), channel_id=1, source_target_pairs={{0,3},{1,2},{2,1},{3,0},{4,7},{5,6},{6,5},{7,4},{8,11},{9,10},{10,... | collective-permute-start | bytes 589832 | tf_op jit(solution)/shard_map/ppermute | solution.py:361
  75.6 15.6 %collective-permute-start.25 = (bf16[128,768]{1,0:T(8,128)(2,1)S(1)}, bf16[128,768]{1,0:T(8,128)(2,1)S(1)}, u32[]{:S(2)}, u32[]{:S(2)}) collective-permute-start(bf16[128,768]{1,0:T(8,128)(2,1)S(1)} %shard_map.78), channel_id=1, source_target_pairs={{0,2},{1,3},{2,0},{3,1},{4,6},{5,7},{6,4},{7,5},{8,10},{9,11},{10,... | collective-permute-start | bytes 589832 | tf_op jit(solution)/shard_map/ppermute | solution.py:361
  77.2 13.9 %collective-permute-start.21 = (bf16[128,768]{1,0:T(8,128)(2,1)S(1)}, bf16[128,768]{1,0:T(8,128)(2,1)S(1)}, u32[]{:S(2)}, u32[]{:S(2)}) collective-permute-start(bf16[128,768]{1,0:T(8,128)(2,1)S(1)} %get-tuple-element.82), channel_id=1, source_target_pairs={{0,8},{4,12},{8,0},{12,4},{1,9},{5,13},{9,1},{13,5},{2,10},{6,14},... | collective-permute-start | bytes 589832 | tf_op jit(solution)/shard_map/ppermute | solution.py:358
  79.8 11.4 %collective-permute-start.28 = (bf16[128,768]{1,0:T(8,128)(2,1)S(1)}, bf16[128,768]{1,0:T(8,128)(2,1)S(1)}, u32[]{:S(2)}, u32[]{:S(2)}) collective-permute-start(bf16[128,768]{1,0:T(8,128)(2,1)S(1)} %shard_map.80), channel_id=1, source_target_pairs={{0,1},{1,0},{2,3},{3,2},{4,5},{5,4},{6,7},{7,6},{8,9},{9,8},{10,11... | collective-permute-start | bytes 589832 | tf_op jit(solution)/shard_map/ppermute | solution.py:361

commit v2 on v1

--- a/solution.py
+++ b/solution.py
@@ -18,7 +18,7 @@
     return (jax.nn.silu(gate) * up).astype(bf16)
 
 
-def plan_kernel(blocks, experts, idx, *refs):
+def plan_kernel(blocks, experts, base, *refs):
     names, (sel_out, back_out, sign_out) = refs[:blocks], refs[blocks:]
     toks = names[0].shape[1]
     ahead = (lax.broadcasted_iota(jnp.int32, (toks, toks), 1) < lax.broadcasted_iota(jnp.int32, (toks, toks), 0)).astype(bf16)
@@ -29,7 +29,7 @@
     for j in range(blocks):
         pair = names[j][...]
         for e in range(experts):
-            own = idx[0] + e
+            own = base[0] + e
             mine = (pair[0:1] == own) | (pair[1:2] == own)
             flag = mine.astype(f32)
             wide = jnp.broadcast_to(flag, (8, toks)).astype(bf16)
@@ -45,7 +45,7 @@
             sign_out[j, e] = (num == own).astype(f32) - (num == other).astype(f32)
 
 
-def plan(base, names, experts, count):
+def plan(table, names, experts, count):
     blocks, toks = len(names), names[0].shape[1]
     return pl.pallas_call(
         functools.partial(plan_kernel, blocks, experts),
@@ -58,10 +58,11 @@
         out_specs=(VM, VM, VM),
         compiler_params=pltpu.CompilerParams(vmem_limit_bytes=4 << 20),
         cost_estimate=pl.CostEstimate(flops=1 << 24, bytes_accessed=1 << 18, transcendentals=0),
-    )(base.reshape(1).astype(jnp.int32), *names)
-
-
-def plan_plain(base, names, experts, count):
+    )(table[-1], *names)
+
+
+def plan_plain(table, names, experts, count):
+    base = table[-1][0]
     names = jnp.stack(names)
     blocks, _, toks = names.shape
     here = base + jnp.arange(experts, dtype=jnp.int32)
@@ -77,13 +78,9 @@
     return sel, sel.swapaxes(1, 2), (num == own).astype(f32) - (num == other).astype(f32)
 
 
-def fetch_up(wg, wu, block, kb, out, sem):
+def fetch_up(wg, wu, block, kb, out, sem, expert):
     at = pl.ds(pl.multiple_of(block * kb, 128), kb)
-    copies = []
-    for e in range(wg.shape[0]):
-        for m, w in enumerate((wg, wu)):
-            copies.append(pltpu.make_async_copy(w.at[e, at], out.at[e, m], sem.at[e, m]))
-    return copies
+    return [pltpu.make_async_copy(w.at[expert, at], out.at[m], sem.at[m]) for m, w in enumerate((wg, wu))]
 
 
 def fetch_down(wd, block, kb, out, sem):
@@ -97,41 +94,42 @@
     return copies
 
 
-def first_kernel(idx, tokens, router, wg, wu, tok_out, router_out, w_out, sem, small):
+def first_kernel(count, *refs):
+    idx, (tokens, router, wg, wu, tok_out, router_out, w_out, sem, small) = refs[0], refs[count:]
     copies = [
         pltpu.make_async_copy(tokens, tok_out, small.at[0]),
         pltpu.make_async_copy(router, router_out, small.at[1]),
-    ] + fetch_up(wg, wu, idx[0], tokens.shape[1], w_out, sem)
+    ] + fetch_up(wg, wu, idx[0], tokens.shape[1], w_out, sem, 0)
     for c in copies:
         c.start()
     for c in copies:
         c.wait()
 
 
-def first_fetch(block, tokens, router, wg, wu):
-    experts, _, ff = wg.shape
+def first_fetch(table, tokens, router, wg, wu):
+    ff = wg.shape[2]
     kb = tokens.shape[1]
     return pl.pallas_call(
-        first_kernel,
+        functools.partial(first_kernel, len(table)),
         out_shape=(
             jax.ShapeDtypeStruct(tokens.shape, bf16),
             jax.ShapeDtypeStruct(router.shape, bf16),
-            jax.ShapeDtypeStruct((experts, 2, kb, ff), bf16),
+            jax.ShapeDtypeStruct((2, kb, ff), bf16),
         ),
-        in_specs=[SM, ANY, ANY, ANY, ANY],
+        in_specs=[SM] * len(table) + [ANY] * 4,
         out_specs=(VM, VM, VM),
-        scratch_shapes=[pltpu.SemaphoreType.DMA((experts, 2)), pltpu.SemaphoreType.DMA((2,))],
+        scratch_shapes=[pltpu.SemaphoreType.DMA((2,)), pltpu.SemaphoreType.DMA((2,))],
         compiler_params=pltpu.CompilerParams(vmem_limit_bytes=1 << 20),
-        cost_estimate=pl.CostEstimate(flops=0, bytes_accessed=4 * experts * kb * ff, transcendentals=0),
-    )(block.reshape(1).astype(jnp.int32), tokens, router, wg, wu)
+        cost_estimate=pl.CostEstimate(flops=0, bytes_accessed=4 * kb * ff, transcendentals=0),
+    )(*table, tokens, router, wg, wu)
 
 
 def up_kernel(first, last, blocks, experts, *refs):
-    idx, refs = refs[0], list(refs[1:])
+    idx, refs = [r[0] for r in refs[:2]], list(refs[2:])
     xs, refs = refs[:blocks], refs[blocks:]
-    sel, router, now = refs[:3]
-    ahead = refs[3:4] if last else refs[3:5]
-    refs = refs[4:] if last else refs[5:]
+    sel, router, now, wg, wu = refs[:5]
+    ahead = refs[5:6] if last else (wg, wu)
+    refs = refs[6:] if last else refs[5:]
     if not first:
         g_in, u_in, l_in = refs[:3]
         refs = refs[3:]
@@ -141,12 +139,13 @@
     else:
         g_out, u_out, l_out, w_out = refs[:4]
         refs = refs[4:]
-    rows, sem = refs
+    rows, sem, buf, own = refs
     kb = rows.shape[2]
-    fetch = fetch_down if last else fetch_up
-    copies = fetch(*ahead, idx[1], kb, w_out, sem)
-    for c in copies:
-        c.start()
+    mine = [fetch_up(wg, wu, idx[0], kb, buf.at[e - 1], own.at[e - 1], e) for e in range(1, experts)]
+    copies = fetch_down(*ahead, idx[1], kb, w_out, sem) if last else fetch_up(*ahead, idx[1], kb, w_out, sem, 0)
+    for pair in mine:
+        for c in pair:
+            c.start()
     rt = router[:, pl.ds(pl.multiple_of(idx[0] * kb, 128), kb)]
     for j in range(blocks):
         x = xs[j][...]
@@ -162,15 +161,16 @@
             w = jax.nn.sigmoid(jnp.sum(sign[j, e] * lt, axis=0, keepdims=True))
             at = sel[j, e * CAP : (e + 1) * CAP].astype(f32)
             s_out[e, j * CAP : (j + 1) * CAP] = jnp.sum(at * w, axis=1, keepdims=True)
-    n_all = now.shape[3]
+    n_all = now.shape[2]
     step = min(512, n_all)
-
-    def column(i, carry):
-        e = i // (n_all // step)
-        sl = pl.ds(pl.multiple_of(i % (n_all // step) * step, step), step)
+    turns = n_all // step
+
+    def column(e, i, carry):
+        sl = pl.ds(pl.multiple_of(i * step, step), step)
         x = rows[e]
-        g = jnp.dot(x, now[e, 0, :, sl], preferred_element_type=f32)
-        u = jnp.dot(x, now[e, 1, :, sl], preferred_element_type=f32)
+        w = now if e == 0 else buf.at[e - 1]
+        g = jnp.dot(x, w[0, :, sl], preferred_element_type=f32)
+        u = jnp.dot(x, w[1, :, sl], preferred_element_type=f32)
         if not first:
             g = g_in[e, :, sl] + g
             u = u_in[e, :, sl] + u
@@ -181,13 +181,24 @@
             u_out[e, :, sl] = u
         return carry
 
-    lax.fori_loop(0, experts * (n_all // step), column, 0)
+    for e in range(experts):
+        if e:
+            for c in mine[e - 1]:
+                c.wait()
+        begin = 0
+        if e == max(0, experts - 2):
+            begin = turns // 2 if experts > 1 else 0
+            lax.fori_loop(0, begin, functools.partial(column, e), 0)
+            for c in copies:
+                c.start()
+        lax.fori_loop(begin, turns, functools.partial(column, e), 0)
     for c in copies:
         c.wait()
 
 
-def up_chunk(block, after, xs, sel, sign, router, now, ahead, acc, last):
-    experts, _, kb, ff = now.shape
+def up_chunk(table, spots, xs, sel, sign, router, now, ahead, acc, last):
+    experts, _, ff = ahead[0].shape
+    kb = xs[0].shape[1]
     blocks = len(xs)
     slots = blocks * CAP
     first = acc is None
@@ -201,18 +212,22 @@
         )
     else:
         out = (big, big, lo, jax.ShapeDtypeStruct(now.shape, bf16))
-    idx = jnp.stack([block, after]).astype(jnp.int32)
-    args = [idx, *xs, sel, router, now, *ahead] + ([] if first else list(acc)) + ([sign] if last else [])
-    n0 = 1 + blocks + 3 + len(ahead)
+    args = [*(table[i] for i in spots), *xs, sel, router, now, *ahead] + ([] if first else list(acc)) + ([sign] if last else [])
+    n0 = 2 + blocks + 3 + len(ahead)
     alias = {} if first or last else {n0: 0, n0 + 1: 1, n0 + 2: 2}
     return pl.pallas_call(
         functools.partial(up_kernel, first, last, blocks, experts),
         out_shape=out,
-        in_specs=[SM] + [VM] * blocks + [VM] * 3 + [ANY] * len(ahead) + ([] if first else [VM] * 3) + ([VM] if last else []),
+        in_specs=[SM, SM] + [VM] * blocks + [VM] * 3 + [ANY] * len(ahead) + ([] if first else [VM] * 3) + ([VM] if last else []),
         out_specs=tuple([VM] * len(out)),
-        scratch_shapes=[pltpu.VMEM((experts, slots, kb), bf16), pltpu.SemaphoreType.DMA((experts, 2))],
+        scratch_shapes=[
+            pltpu.VMEM((experts, slots, kb), bf16),
+            pltpu.SemaphoreType.DMA((experts, 2) if last else (2,)),
+            pltpu.VMEM((max(1, experts - 1), 2, kb, ff), bf16),
+            pltpu.SemaphoreType.DMA((max(1, experts - 1), 2)),
+        ],
         input_output_aliases=alias,
-        compiler_params=pltpu.CompilerParams(vmem_limit_bytes=2 << 20),
+        compiler_params=pltpu.CompilerParams(vmem_limit_bytes=(2 << 20) + 4 * max(1, experts - 1) * kb * ff),
         cost_estimate=pl.CostEstimate(
             flops=4 * experts * slots * kb * ff,
             bytes_accessed=4 * experts * kb * ff,
@@ -270,13 +285,13 @@
         c.wait()
 
 
-def down_chunk(after, h, back, wslot, now, wd, gate):
+def down_chunk(table, spot, h, back, wslot, now, wd, gate):
     experts, slots, ff = h.shape
     blocks, toks, _ = back.shape
     kb = now.shape[2]
-    last = after is None
+    last = spot is None
     out = (jax.ShapeDtypeStruct((blocks // 2, toks, kb), bf16),) * 2
-    args = [jnp.zeros((1,), jnp.int32) if last else after.reshape(1).astype(jnp.int32), h, back, wslot, now, gate]
+    args = [table[0 if last else spot], h, back, wslot, now, gate]
     return pl.pallas_call(
         functools.partial(down_kernel, experts, blocks, last),
         out_shape=out if last else out + (jax.ShapeDtypeStruct(now.shape, bf16),),
@@ -349,6 +364,8 @@
     toks, kb = tokens.shape
     e_at = lax.axis_index("expert")
     h_at = lax.axis_index("hidden")
+    table = [(h_at ^ k).astype(jnp.int32).reshape(1) for k in range(nh)]
+    table.append((e_at * experts).astype(jnp.int32).reshape(1))
     kernels = kb % 128 == 0 and toks % 128 == 0
 
     def over_core(v):
@@ -386,40 +403,43 @@
         gate_weight, up_weight, down_weight = (
             pltpu.with_memory_space_constraint(w, pltpu.HBM) for w in (gate_weight, up_weight, down_weight)
         )
-        held, router, weights = first_fetch(h_at, tokens, router, gate_weight, up_weight)
+        local = tokens
+        router = pltpu.with_memory_space_constraint(router, pltpu.HBM)
+        held, router, weights = first_fetch(table, local, router, gate_weight, up_weight)
     else:
         held = tokens
 
     planned = plan if kernels else plan_plain
-    sel, back, sign = planned(e_at * experts, names, experts, router_weight.shape[1])
+    sel, back, sign = planned(table, names, experts, router_weight.shape[1])
 
     down_order = [k for k in range(nh - 1, 0, -1)] + [0]
     acc = None
     small = []
     for at, k in enumerate(order):
         if kernels and at >= 2:
-            slices[k], small[at - 2] = lax.optimization_barrier((slices[k], small[at - 2]))
+            back_at = max(0, at - 3)
+            slices[k], small[back_at] = lax.optimization_barrier((slices[k], small[back_at]))
         xs = spread(slices[k], held if k == 0 else None)
         last = at == nh - 1
         if kernels:
-            after = h_at ^ (down_order[0] if last else order[at + 1])
-            ahead = (down_weight,) if last else (gate_weight, up_weight)
-            *acc, weights = up_chunk(h_at ^ k, after, xs, sel, sign, router, weights, ahead, acc, last)
+            spots = (k, down_order[0] if last else order[at + 1])
+            ahead = (gate_weight, up_weight) + ((down_weight,) if last else ())
+            *acc, weights = up_chunk(table, spots, xs, sel, sign, router, weights, ahead, acc, last)
             small.append(acc[-1])
         else:
-            acc = up_chunk_plain(h_at ^ k, xs, sel, sign, router, gate_weight, up_weight, acc, last)
+            acc = up_chunk_plain(table[k][0], xs, sel, sign, router, gate_weight, up_weight, acc, last)
     h, wslot = acc
 
     total = []
     sent = []
     for at, k in enumerate(down_order):
         if kernels:
-            after = None if at == nh - 1 else h_at ^ down_order[at + 1]
+            spot = None if at == nh - 1 else down_order[at + 1]
             gate = sent[at - 2] if at >= 2 else wslot
-            keep, send, *more = down_chunk(after, h, back, wslot, weights, down_weight, gate)
+            keep, send, *more = down_chunk(table, spot, h, back, wslot, weights, down_weight, gate)
             weights = more[0] if more else None
         else:
-            keep, send = down_chunk_plain(h_at ^ k, h, back, wslot, down_weight, kb)
+            keep, send = down_chunk_plain(table[k][0], h, back, wslot, down_weight, kb)
         got = over_core(send)
         if kernels:
             base, *outs = pair_sum(keep, got)

time: 92.1 us -> 93.7 us (1.017)
  waiting for transfers between devices: 25.6 us -> 31.1 us
  Pallas kernels: 38.1 us -> 35.3 us
    ppermute x9, waiting for transfers between devices: 16.1 us -> 18.7 us  [over_x(): return lax.ppermute(v, 'expert', [(i, i ^ 2 * d) for i in range(blocks)])]
    pallas_call x1, Pallas kernels: 4.99 us -> 3.14 us  [first_fetch(): pl.pallas_call(functools.partial(first_kernel, len(table)), out_shape=(ja...]
    ppermute x6, waiting for transfers between devices: 9.5 us -> 11 us  [over_z(): return lax.ppermute(v, 'hidden', [(i, i ^ k) for i in range(nh)])]
    ppermute x14, waiting for transfers between devices: 0.04 us -> 1.4 us  [over_core(): return lax.ppermute(v, 'expert', [(i, i ^ 1) for i in range(blocks)])]
    ppermute x14, starting transfers between devices: 3.18 us -> 2.04 us  [over_core(): return lax.ppermute(v, 'expert', [(i, i ^ 1) for i in range(blocks)])]
    pallas_call x4, Pallas kernels: 21.5 us -> 20.5 us  [up_chunk(): pl.pallas_call(functools.partial(up_kernel, first, last, blocks, experts)...]
  transfers between devices with their start and end apart: 29 -> 29, of which waited for: 6 -> 10; matrix products, arithmetic and copies ran while one was open for 0% -> 0% of each run, Pallas kernels for 33% -> 29%
where the time goes in v2:
time: 93.7 us; the launch traced here: 93.6 us
  Pallas kernels  35.3 us (38%)
  waiting for transfers between devices  31.1 us (33%)
  starting transfers between devices  25.3 us (27%)
    pallas_call x4, Pallas kernels, up_chunk(): pl.pallas_call(functools.partial(up_kernel, first, last, blocks, experts)...  20.5 us
    ppermute x9, waiting for transfers between devices, over_x(): return lax.ppermute(v, 'expert', [(i, i ^ 2 * d) for i in range(blocks)])  18.7 us
    ppermute x9, starting transfers between devices, over_x(): return lax.ppermute(v, 'expert', [(i, i ^ 2 * d) for i in range(blocks)])  11.9 us
    ppermute x6, starting transfers between devices, over_z(): return lax.ppermute(v, 'hidden', [(i, i ^ k) for i in range(nh)])  11.3 us
    ppermute x6, waiting for transfers between devices, over_z(): return lax.ppermute(v, 'hidden', [(i, i ^ k) for i in range(nh)])  11 us
    pallas_call x4, Pallas kernels, down_chunk(): pl.pallas_call(functools.partial(down_kernel, experts, blocks, last), out...  10.7 us
    pallas_call x1, Pallas kernels, first_fetch(): pl.pallas_call(functools.partial(first_kernel, len(table)), out_shape=(ja...  3.14 us
    ppermute x14, starting transfers between devices, over_core(): return lax.ppermute(v, 'expert', [(i, i ^ 1) for i in range(blocks)])  2.04 us
  transfers between devices with their start and end apart: 29, of which 10 were waited for; matrix products, arithmetic and copies ran while one was open for 0% of the time, Pallas kernels for 29%

profile of v2, /device:TPU:0, one launch (start us, length us, event | category | flops | bytes accessed | tf_op | source)
XLA Modules:
  0.0 93.6 jit_solution(12955442895909312174)
XLA Ops:
  0.0 3.0 %collective-permute-start.9 = (bf16[128,768]{1,0:T(8,128)(2,1)}, bf16[128,768]{1,0:T(8,128)(2,1)S(1)}, u32[]{:S(2)}, u32[]{:S(2)}) collective-permute-start(bf16[128,768]{1,0:T(8,128)(2,1)} %refs_5_.1), channel_id=1, source_target_pairs={{0,8},{4,12},{8,0},{12,4},{1,9},{5,13},{9,1},{13,5},{2,10},{6,14},... | collective-permute-start | bytes 589832 | tf_op jit(solution)/shard_map/ppermute | solution.py:375
  3.0 1.6 %collective-permute-start.14 = (bf16[128,768]{1,0:T(8,128)(2,1)}, bf16[128,768]{1,0:T(8,128)(2,1)S(1)}, u32[]{:S(2)}, u32[]{:S(2)}) collective-permute-start(bf16[128,768]{1,0:T(8,128)(2,1)} %refs_5_.1), channel_id=1, source_target_pairs={{0,1},{1,0},{2,3},{3,2},{4,5},{5,4},{6,7},{7,6},{8,9},{9,8},{10,11... | collective-permute-start | bytes 589832 | tf_op jit(solution)/shard_map/ppermute | solution.py:378
  4.5 2.5 %collective-permute-start = (bf16[128,768]{1,0:T(8,128)(2,1)}, bf16[128,768]{1,0:T(8,128)(2,1)S(1)}, u32[]{:S(2)}, u32[]{:S(2)}) collective-permute-start(bf16[128,768]{1,0:T(8,128)(2,1)} %refs_5_.1), channel_id=1, source_target_pairs={{0,3},{1,2},{2,1},{3,0},{4,7},{5,6},{6,5},{7,4},{8,11},{9,10},{10,... | collective-permute-start | bytes 589832 | tf_op jit(solution)/shard_map/ppermute | solution.py:378
  7.0 1.1 %collective-permute-done.9.refs_4_ = bf16[128,768]{1,0:T(8,128)(2,1)S(1)} collective-permute-done((bf16[128,768]{1,0:T(8,128)(2,1)}, bf16[128,768]{1,0:T(8,128)(2,1)S(1)}, u32[]{:S(2)}, u32[]{:S(2)}) %collective-permute-start.9) | collective-permute-done | bytes 196640 | tf_op jit(solution)/shard_map/ppermute | solution.py:375
  8.1 1.7 %collective-permute-start.6 = (s32[2,128]{1,0:T(2,128)}, s32[2,128]{1,0:T(2,128)S(1)}, u32[]{:S(2)}, u32[]{:S(2)}) collective-permute-start(s32[2,128]{1,0:T(2,128)} %bitcast.7), channel_id=1, source_target_pairs={{0,8},{4,12},{8,0},{12,4},{1,9},{5,13},{9,1},{13,5},{2,10},{6,14},... | collective-permute-start | bytes 3080 | tf_op jit(solution)/shard_map/ppermute | solution.py:375
  9.8 2.0 %collective-permute-done.6.refs_2_ = s32[2,128]{1,0:T(2,128)S(1)} collective-permute-done((s32[2,128]{1,0:T(2,128)}, s32[2,128]{1,0:T(2,128)S(1)}, u32[]{:S(2)}, u32[]{:S(2)}) %collective-permute-start.6) | collective-permute-done | bytes 1056 | tf_op jit(solution)/shard_map/ppermute | solution.py:375
  11.9 1.4 %collective-permute-done.5.refs_1_ = s32[2,128]{1,0:T(2,128)S(1)} collective-permute-done((s32[2,128]{1,0:T(2,128)}, s32[2,128]{1,0:T(2,128)S(1)}, u32[]{:S(2)}, u32[]{:S(2)}) %collective-permute-start.5) | collective-permute-done | bytes 1056 | tf_op jit(solution)/shard_map/ppermute | solution.py:372
  13.4 0.9 copy-done
  14.3 3.1 %shard_map.65 = (bf16[128,768]{1,0:T(8,128)(2,1)S(1)}, bf16[8,3072]{1,0:T(8,128)(2,1)S(1)}, bf16[2,768,2048]{2,1,0:T(8,128)(2,1)S(1)}) custom-call(s32[1]{0:T(128)} %bitcast.refs_0_, s32[1]{0:T(128)} %bitcast.5.refs_1_.refs_0_, s32[1]{0:T(128)} %bitcast.1.refs_2_.refs_1_.refs_0_, s32[1]{0:T(128)} %bitcast.2.refs_3_.refs_1_.refs_0_, s32[1]{0:T(128)} %bitcast.3.base.refs_4_, ...), custom_call_target="tpu_custom_call" | custom-call | bytes 6291456 | tf_op jit(solution)/shard_map/pallas_call | solution.py:112
  18.0 1.8 %collective-permute-start.16 = (bf16[128,768]{1,0:T(8,128)(2,1)S(1)}, bf16[128,768]{1,0:T(8,128)(2,1)S(1)}, u32[]{:S(2)}, u32[]{:S(2)}) collective-permute-start(bf16[128,768]{1,0:T(8,128)(2,1)S(1)} %collective-permute-done.14.refs_2_), channel_id=1, source_target_pairs={{0,8},{4,12},{8,0},{12,4},{1,9},{5,13},{9,1},{13,5},{2,10},{6,14},... | collective-permute-start | bytes 589832 | tf_op jit(solution)/shard_map/ppermute | solution.py:375
  19.9 1.6 %collective-permute-start.1 = (bf16[128,768]{1,0:T(8,128)(2,1)S(1)}, bf16[128,768]{1,0:T(8,128)(2,1)S(1)}, u32[]{:S(2)}, u32[]{:S(2)}) collective-permute-start(bf16[128,768]{1,0:T(8,128)(2,1)S(1)} %collective-permute-done.refs_2_), channel_id=1, source_target_pairs={{0,1},{1,0},{2,3},{3,2},{4,5},{5,4},{6,7},{7,6},{8,9},{9,8},{10,11... | collective-permute-start | bytes 589832 | tf_op jit(solution)/shard_map/ppermute | solution.py:378
  21.5 5.1 %shard_map.66 = (f32[2,192,2048]{2,1,0:T(8,128)S(1)}, f32[2,192,2048]{2,1,0:T(8,128)S(1)}, f32[4,8,128]{2,1,0:T(8,128)S(1)}, bf16[2,768,2048]{2,1,0:T(8,128)(2,1)S(1)}) custom-call(s32[1]{0:T(128)} %bitcast.refs_0_, s32[1]{0:T(128)} %bitcast.5.refs_1_.refs_0_, bf16[128,768]{1,0:T(8,128)(2,1)S(1)} %get-tuple-element.48.refs_2_, ...), custom_call_target="tpu_custom_call" | custom-call | flops 2415919104 | bytes 12582912 | tf_op jit(solution)/shard_map/pallas_call | solution.py:218
  26.6 0.6 collective-permute-start.12
  27.2 1.5 %collective-permute-start.3 = (bf16[128,768]{1,0:T(8,128)(2,1)S(1)}, bf16[128,768]{1,0:T(8,128)(2,1)S(1)}, u32[]{:S(2)}, u32[]{:S(2)}) collective-permute-start(bf16[128,768]{1,0:T(8,128)(2,1)S(1)} %collective-permute-done.1.refs_2_), channel_id=1, source_target_pairs={{0,8},{4,12},{8,0},{12,4},{1,9},{5,13},{9,1},{13,5},{2,10},{6,14},... | collective-permute-start | bytes 589832 | tf_op jit(solution)/shard_map/ppermute | solution.py:375
  29.2 5.2 %collective-permute-done.12.refs_4_ = bf16[128,768]{1,0:T(8,128)(2,1)S(1)} collective-permute-done((bf16[128,768]{1,0:T(8,128)(2,1)S(1)}, bf16[128,768]{1,0:T(8,128)(2,1)S(1)}, u32[]{:S(2)}, u32[]{:S(2)}) %collective-permute-start.12) | collective-permute-done | bytes 196640 | tf_op jit(solution)/shard_map/ppermute | solution.py:375
  34.4 3.4 %collective-permute-done.3.refs_4_ = bf16[128,768]{1,0:T(8,128)(2,1)S(1)} collective-permute-done((bf16[128,768]{1,0:T(8,128)(2,1)S(1)}, bf16[128,768]{1,0:T(8,128)(2,1)S(1)}, u32[]{:S(2)}, u32[]{:S(2)}) %collective-permute-start.3) | collective-permute-done | bytes 196640 | tf_op jit(solution)/shard_map/ppermute | solution.py:375
  37.8 5.0 %shard_map.67 = (f32[2,192,2048]{2,1,0:T(8,128)S(1)}, f32[2,192,2048]{2,1,0:T(8,128)S(1)}, f32[4,8,128]{2,1,0:T(8,128)S(1)}, bf16[2,768,2048]{2,1,0:T(8,128)(2,1)S(1)}) custom-call(s32[1]{0:T(128)} %bitcast.5.refs_1_.refs_0_, s32[1]{0:T(128)} %bitcast.2.refs_3_.refs_1_.refs_0_, ...), custom_call_target="tpu_custom_call", output_to_operand_aliasing={{0}: (11, {}), {1}: (12, {}), {2}: (13, {})} | custom-call | flops 2415919104 | bytes 12582912 | tf_op jit(solution)/shard_map/pallas_call | solution.py:218
  42.9 5.0 %shard_map.68 = (f32[2,192,2048]{2,1,0:T(8,128)S(1)}, f32[2,192,2048]{2,1,0:T(8,128)S(1)}, f32[4,8,128]{2,1,0:T(8,128)S(1)}, bf16[2,768,2048]{2,1,0:T(8,128)(2,1)S(1)}) custom-call(s32[1]{0:T(128)} %bitcast.2.refs_3_.refs_1_.refs_0_, s32[1]{0:T(128)} %bitcast.1.refs_2_.refs_1_.refs_0_, ...), custom_call_target="tpu_custom_call", output_to_operand_aliasing={{0}: (11, {}), {1}: (12, {}), {2}: (13, {})} | custom-call | flops 2415919104 | bytes 12582912 | tf_op jit(solution)/shard_map/pallas_call | solution.py:218
  47.9 5.4 %shard_map.69 = (bf16[2,192,2048]{2,1,0:T(8,128)(2,1)S(1)}, f32[2,192,1]{2,1,0:T(8,128)S(1)}, bf16[2,2048,768]{2,1,0:T(8,128)(2,1)S(1)}) custom-call(s32[1]{0:T(128)} %bitcast.1.refs_2_.refs_1_.refs_0_, s32[1]{0:T(128)} %bitcast.2.refs_3_.refs_1_.refs_0_, bf16[128,768]{1,0:T(8,128)(2,1)S(1)} %collective-permute-done.1.refs_2_, ...), custom_call_target="tpu_custom_call" | custom-call | flops 2415919104 | bytes 12582912 | tf_op jit(solution)/shard_map/pallas_call | solution.py:218
  53.4 2.9 %shard_map.70 = (bf16[2,128,768]{2,1,0:T(8,128)(2,1)S(1)}, bf16[2,128,768]{2,1,0:T(8,128)(2,1)S(1)}, bf16[2,2048,768]{2,1,0:T(8,128)(2,1)S(1)}) custom-call(s32[1]{0:T(128)} %bitcast.1.refs_2_.refs_1_.refs_0_, bf16[2,192,2048]{2,1,0:T(8,128)(2,1)S(1)} %get-tuple-element.64.refs_1_, bf16[4,128,96]{2,1,0:T(8,128)(2,1)S(1)} %get-tuple-element.65.refs_2_, ...), custom_call_target="tpu_custom_call" | custom-call | flops 1207959552 | bytes 6291456 | tf_op jit(solution)/shard_map/pallas_call | solution.py:295
  56.8 2.9 %shard_map.71 = (bf16[2,128,768]{2,1,0:T(8,128)(2,1)S(1)}, bf16[2,128,768]{2,1,0:T(8,128)(2,1)S(1)}, bf16[2,2048,768]{2,1,0:T(8,128)(2,1)S(1)}) custom-call(s32[1]{0:T(128)} %bitcast.5.refs_1_.refs_0_, bf16[2,192,2048]{2,1,0:T(8,128)(2,1)S(1)} %get-tuple-element.64.refs_1_, bf16[4,128,96]{2,1,0:T(8,128)(2,1)S(1)} %get-tuple-element.65.refs_2_, ...), custom_call_target="tpu_custom_call" | custom-call | flops 1207959552 | bytes 6291456 | tf_op jit(solution)/shard_map/pallas_call | solution.py:295
  59.9 2.9 %shard_map.73 = (bf16[2,128,768]{2,1,0:T(8,128)(2,1)S(1)}, bf16[2,128,768]{2,1,0:T(8,128)(2,1)S(1)}, bf16[2,2048,768]{2,1,0:T(8,128)(2,1)S(1)}) custom-call(s32[1]{0:T(128)} %bitcast.refs_0_, bf16[2,192,2048]{2,1,0:T(8,128)(2,1)S(1)} %get-tuple-element.64.refs_1_, bf16[4,128,96]{2,1,0:T(8,128)(2,1)S(1)} %get-tuple-element.65.refs_2_, ...), custom_call_target="tpu_custom_call" | custom-call | flops 1207959552 | bytes 6291456 | tf_op jit(solution)/shard_map/pallas_call | solution.py:295
  63.5 2.0 %shard_map.75 = (bf16[2,128,768]{2,1,0:T(8,128)(2,1)S(1)}, bf16[2,128,768]{2,1,0:T(8,128)(2,1)S(1)}) custom-call(s32[1]{0:T(128)} %bitcast.refs_0_, bf16[2,192,2048]{2,1,0:T(8,128)(2,1)S(1)} %get-tuple-element.64.refs_1_, bf16[4,128,96]{2,1,0:T(8,128)(2,1)S(1)} %get-tuple-element.65.refs_2_, f32[2,192,1]{2,1,0:T(8,128)S(1)} %get-tuple-element.66.refs_3_.refs_5_, ...), custom_call_target="tpu_custom_call" | custom-call | flops 1207959552 | bytes 6291456 | tf_op jit(solution)/shard_map/pallas_call | solution.py:295
  66.1 1.5 %collective-permute-start.24 = (bf16[128,768]{1,0:T(8,128)(2,1)S(1)}, bf16[128,768]{1,0:T(8,128)(2,1)S(1)}, u32[]{:S(2)}, u32[]{:S(2)}) collective-permute-start(bf16[128,768]{1,0:T(8,128)(2,1)S(1)} %get-tuple-element.76.refs_5_), channel_id=1, source_target_pairs={{0,8},{4,12},{8,0},{12,4},{1,9},{5,13},{9,1},{13,5},{2,10},{6,14},... | collective-permute-start | bytes 589832 | tf_op jit(solution)/shard_map/ppermute | solution.py:375
  67.7 0.6 collective-permute-start.27
  68.3 5.0 %collective-permute-done.22.refs_0_ = bf16[128,768]{1,0:T(8,128)(2,1)S(1)} collective-permute-done((bf16[128,768]{1,0:T(8,128)(2,1)S(1)}, bf16[128,768]{1,0:T(8,128)(2,1)S(1)}, u32[]{:S(2)}, u32[]{:S(2)}) %collective-permute-start.22) | collective-permute-done | bytes 196640 | tf_op jit(solution)/shard_map/ppermute | solution.py:375
  73.4 2.5 %collective-permute-start.23 = (bf16[128,768]{1,0:T(8,128)(2,1)S(1)}, bf16[128,768]{1,0:T(8,128)(2,1)S(1)}, u32[]{:S(2)}, u32[]{:S(2)}) collective-permute-start(bf16[128,768]{1,0:T(8,128)(2,1)S(1)} %shard_map.77), channel_id=1, source_target_pairs={{0,3},{1,2},{2,1},{3,0},{4,7},{5,6},{6,5},{7,4},{8,11},{9,10},{10,... | collective-permute-start | bytes 589832 | tf_op jit(solution)/shard_map/ppermute | solution.py:378
  75.9 1.6 %collective-permute-done.24.refs_0_ = bf16[128,768]{1,0:T(8,128)(2,1)S(1)} collective-permute-done((bf16[128,768]{1,0:T(8,128)(2,1)S(1)}, bf16[128,768]{1,0:T(8,128)(2,1)S(1)}, u32[]{:S(2)}, u32[]{:S(2)}) %collective-permute-start.24) | collective-permute-done | bytes 196640 | tf_op jit(solution)/shard_map/ppermute | solution.py:375
  77.6 2.7 %collective-permute-start.25 = (bf16[128,768]{1,0:T(8,128)(2,1)S(1)}, bf16[128,768]{1,0:T(8,128)(2,1)S(1)}, u32[]{:S(2)}, u32[]{:S(2)}) collective-permute-start(bf16[128,768]{1,0:T(8,128)(2,1)S(1)} %shard_map.78), channel_id=1, source_target_pairs={{0,2},{1,3},{2,0},{3,1},{4,6},{5,7},{6,4},{7,5},{8,10},{9,11},{10,... | collective-permute-start | bytes 589832 | tf_op jit(solution)/shard_map/ppermute | solution.py:378
  80.4 0.6 collective-permute-start.21
  82.3 10.5 %collective-permute-done.25 = bf16[128,768]{1,0:T(8,128)(2,1)S(1)} collective-permute-done((bf16[128,768]{1,0:T(8,128)(2,1)S(1)}, bf16[128,768]{1,0:T(8,128)(2,1)S(1)}, u32[]{:S(2)}, u32[]{:S(2)}) %collective-permute-start.25) | collective-permute-done | bytes 196640 | tf_op jit(solution)/shard_map/ppermute | solution.py:378
  92.8 0.8 add_convert_fusion
  (48 shorter events, 4.9 us)
Async XLA Ops:
  0.0 8.1 %collective-permute-start.9 = (bf16[128,768]{1,0:T(8,128)(2,1)}, bf16[128,768]{1,0:T(8,128)(2,1)S(1)}, u32[]{:S(2)}, u32[]{:S(2)}) collective-permute-start(bf16[128,768]{1,0:T(8,128)(2,1)} %refs_5_.1), channel_id=1, source_target_pairs={{0,8},{4,12},{8,0},{12,4},{1,9},{5,13},{9,1},{13,5},{2,10},{6,14},... | collective-permute-start | bytes 589832 | tf_op jit(solution)/shard_map/ppermute | solution.py:375
  3.0 15.1 %collective-permute-start.14 = (bf16[128,768]{1,0:T(8,128)(2,1)}, bf16[128,768]{1,0:T(8,128)(2,1)S(1)}, u32[]{:S(2)}, u32[]{:S(2)}) collective-permute-start(bf16[128,768]{1,0:T(8,128)(2,1)} %refs_5_.1), channel_id=1, source_target_pairs={{0,1},{1,0},{2,3},{3,2},{4,5},{5,4},{6,7},{7,6},{8,9},{9,8},{10,11... | collective-permute-start | bytes 589832 | tf_op jit(solution)/shard_map/ppermute | solution.py:378
  4.5 15.4 %collective-permute-start = (bf16[128,768]{1,0:T(8,128)(2,1)}, bf16[128,768]{1,0:T(8,128)(2,1)S(1)}, u32[]{:S(2)}, u32[]{:S(2)}) collective-permute-start(bf16[128,768]{1,0:T(8,128)(2,1)} %refs_5_.1), channel_id=1, source_target_pairs={{0,3},{1,2},{2,1},{3,0},{4,7},{5,6},{6,5},{7,4},{8,11},{9,10},{10,... | collective-permute-start | bytes 589832 | tf_op jit(solution)/shard_map/ppermute | solution.py:378
  7.0 14.5 %collective-permute-start.8 = (bf16[128,768]{1,0:T(8,128)(2,1)}, bf16[128,768]{1,0:T(8,128)(2,1)S(1)}, u32[]{:S(2)}, u32[]{:S(2)}) collective-permute-start(bf16[128,768]{1,0:T(8,128)(2,1)} %refs_5_.1), channel_id=1, source_target_pairs={{0,4},{4,0},{8,12},{12,8},{1,5},{5,1},{9,13},{13,9},{2,6},{6,2},{1... | collective-permute-start | bytes 589832 | tf_op jit(solution)/shard_map/ppermute | solution.py:372
  8.1 13.4 %collective-permute-start.10 = (bf16[128,768]{1,0:T(8,128)(2,1)S(1)}, bf16[128,768]{1,0:T(8,128)(2,1)S(1)}, u32[]{:S(2)}, u32[]{:S(2)}) collective-permute-start(bf16[128,768]{1,0:T(8,128)(2,1)S(1)} %collective-permute-done.9.refs_4_), channel_id=1, source_target_pairs={{0,4},{4,0},{8,12},{12,8},{1,5},{5,1},{9,13},{13,9},{2,6},{6,2},{1... | collective-permute-start | bytes 589832 | tf_op jit(solution)/shard_map/ppermute | solution.py:372
  8.1 3.8 %collective-permute-start.6 = (s32[2,128]{1,0:T(2,128)}, s32[2,128]{1,0:T(2,128)S(1)}, u32[]{:S(2)}, u32[]{:S(2)}) collective-permute-start(s32[2,128]{1,0:T(2,128)} %bitcast.7), channel_id=1, source_target_pairs={{0,8},{4,12},{8,0},{12,4},{1,9},{5,13},{9,1},{13,5},{2,10},{6,14},... | collective-permute-start | bytes 3080 | tf_op jit(solution)/shard_map/ppermute | solution.py:375
  11.9 1.4 %collective-permute-start.5 = (s32[2,128]{1,0:T(2,128)}, s32[2,128]{1,0:T(2,128)S(1)}, u32[]{:S(2)}, u32[]{:S(2)}) collective-permute-start(s32[2,128]{1,0:T(2,128)} %bitcast.8), channel_id=1, source_target_pairs={{0,4},{4,0},{8,12},{12,8},{1,5},{5,1},{9,13},{13,9},{2,6},{6,2},{1... | collective-permute-start | bytes 3080 | tf_op jit(solution)/shard_map/ppermute | solution.py:372
  13.2 4.3 %collective-permute-start.7 = (s32[2,128]{1,0:T(2,128)S(1)}, s32[2,128]{1,0:T(2,128)S(1)}, u32[]{:S(2)}, u32[]{:S(2)}) collective-permute-start(s32[2,128]{1,0:T(2,128)S(1)} %collective-permute-done.6.refs_2_), channel_id=1, source_target_pairs={{0,4},{4,0},{8,12},{12,8},{1,5},{5,1},{9,13},{13,9},{2,6},{6,2},{1... | collective-permute-start | bytes 3080 | tf_op jit(solution)/shard_map/ppermute | solution.py:372
  13.4 0.9 copy-start
  14.3 3.2 %copy-start.1 = (s32[128,2]{0,1:T(2,128)S(1)}, s32[128,2]{0,1:T(2,128)}, u32[]{:S(2)}) copy-start(s32[128,2]{0,1:T(2,128)} %param.7) | copy-start | bytes 3076
  18.0 10.6 %collective-permute-start.16 = (bf16[128,768]{1,0:T(8,128)(2,1)S(1)}, bf16[128,768]{1,0:T(8,128)(2,1)S(1)}, u32[]{:S(2)}, u32[]{:S(2)}) collective-permute-start(bf16[128,768]{1,0:T(8,128)(2,1)S(1)} %collective-permute-done.14.refs_2_), channel_id=1, source_target_pairs={{0,8},{4,12},{8,0},{12,4},{1,9},{5,13},{9,1},{13,5},{2,10},{6,14},... | collective-permute-start | bytes 589832 | tf_op jit(solution)/shard_map/ppermute | solution.py:375
  19.8 9.3 %collective-permute-start.15 = (bf16[128,768]{1,0:T(8,128)(2,1)S(1)}, bf16[128,768]{1,0:T(8,128)(2,1)S(1)}, u32[]{:S(2)}, u32[]{:S(2)}) collective-permute-start(bf16[128,768]{1,0:T(8,128)(2,1)S(1)} %collective-permute-done.14.refs_2_), channel_id=1, source_target_pairs={{0,4},{4,0},{8,12},{12,8},{1,5},{5,1},{9,13},{13,9},{2,6},{6,2},{1... | collective-permute-start | bytes 589832 | tf_op jit(solution)/shard_map/ppermute | solution.py:372
  19.9 7.3 %collective-permute-start.1 = (bf16[128,768]{1,0:T(8,128)(2,1)S(1)}, bf16[128,768]{1,0:T(8,128)(2,1)S(1)}, u32[]{:S(2)}, u32[]{:S(2)}) collective-permute-start(bf16[128,768]{1,0:T(8,128)(2,1)S(1)} %collective-permute-done.refs_2_), channel_id=1, source_target_pairs={{0,1},{1,0},{2,3},{3,2},{4,5},{5,4},{6,7},{7,6},{8,9},{9,8},{10,11... | collective-permute-start | bytes 589832 | tf_op jit(solution)/shard_map/ppermute | solution.py:378
  26.6 7.8 %collective-permute-start.12 = (bf16[128,768]{1,0:T(8,128)(2,1)S(1)}, bf16[128,768]{1,0:T(8,128)(2,1)S(1)}, u32[]{:S(2)}, u32[]{:S(2)}) collective-permute-start(bf16[128,768]{1,0:T(8,128)(2,1)S(1)} %collective-permute-done.refs_2_), channel_id=1, source_target_pairs={{0,8},{4,12},{8,0},{12,4},{1,9},{5,13},{9,1},{13,5},{2,10},{6,14},... | collective-permute-start | bytes 589832 | tf_op jit(solution)/shard_map/ppermute | solution.py:375
  27.2 10.7 %collective-permute-start.3 = (bf16[128,768]{1,0:T(8,128)(2,1)S(1)}, bf16[128,768]{1,0:T(8,128)(2,1)S(1)}, u32[]{:S(2)}, u32[]{:S(2)}) collective-permute-start(bf16[128,768]{1,0:T(8,128)(2,1)S(1)} %collective-permute-done.1.refs_2_), channel_id=1, source_target_pairs={{0,8},{4,12},{8,0},{12,4},{1,9},{5,13},{9,1},{13,5},{2,10},{6,14},... | collective-permute-start | bytes 589832 | tf_op jit(solution)/shard_map/ppermute | solution.py:375
  28.7 9.2 %collective-permute-start.17 = (bf16[128,768]{1,0:T(8,128)(2,1)S(1)}, bf16[128,768]{1,0:T(8,128)(2,1)S(1)}, u32[]{:S(2)}, u32[]{:S(2)}) collective-permute-start(bf16[128,768]{1,0:T(8,128)(2,1)S(1)} %collective-permute-done.16.refs_4_), channel_id=1, source_target_pairs={{0,4},{4,0},{8,12},{12,8},{1,5},{5,1},{9,13},{13,9},{2,6},{6,2},{1... | collective-permute-start | bytes 589832 | tf_op jit(solution)/shard_map/ppermute | solution.py:372
  28.7 14.2 %collective-permute-start.11 = (bf16[128,768]{1,0:T(8,128)(2,1)S(1)}, bf16[128,768]{1,0:T(8,128)(2,1)S(1)}, u32[]{:S(2)}, u32[]{:S(2)}) collective-permute-start(bf16[128,768]{1,0:T(8,128)(2,1)S(1)} %collective-permute-done.refs_2_), channel_id=1, source_target_pairs={{0,4},{4,0},{8,12},{12,8},{1,5},{5,1},{9,13},{13,9},{2,6},{6,2},{1... | collective-permute-start | bytes 589832 | tf_op jit(solution)/shard_map/ppermute | solution.py:372
  29.2 18.7 %collective-permute-start.2 = (bf16[128,768]{1,0:T(8,128)(2,1)S(1)}, bf16[128,768]{1,0:T(8,128)(2,1)S(1)}, u32[]{:S(2)}, u32[]{:S(2)}) collective-permute-start(bf16[128,768]{1,0:T(8,128)(2,1)S(1)} %collective-permute-done.1.refs_2_), channel_id=1, source_target_pairs={{0,4},{4,0},{8,12},{12,8},{1,5},{5,1},{9,13},{13,9},{2,6},{6,2},{1... | collective-permute-start | bytes 589832 | tf_op jit(solution)/shard_map/ppermute | solution.py:372
  34.4 8.5 %collective-permute-start.13 = (bf16[128,768]{1,0:T(8,128)(2,1)S(1)}, bf16[128,768]{1,0:T(8,128)(2,1)S(1)}, u32[]{:S(2)}, u32[]{:S(2)}) collective-permute-start(bf16[128,768]{1,0:T(8,128)(2,1)S(1)} %collective-permute-done.12.refs_4_), channel_id=1, source_target_pairs={{0,4},{4,0},{8,12},{12,8},{1,5},{5,1},{9,13},{13,9},{2,6},{6,2},{1... | collective-permute-start | bytes 589832 | tf_op jit(solution)/shard_map/ppermute | solution.py:372
  37.8 10.1 %collective-permute-start.4 = (bf16[128,768]{1,0:T(8,128)(2,1)S(1)}, bf16[128,768]{1,0:T(8,128)(2,1)S(1)}, u32[]{:S(2)}, u32[]{:S(2)}) collective-permute-start(bf16[128,768]{1,0:T(8,128)(2,1)S(1)} %collective-permute-done.3.refs_4_), channel_id=1, source_target_pairs={{0,4},{4,0},{8,12},{12,8},{1,5},{5,1},{9,13},{13,9},{2,6},{6,2},{1... | collective-permute-start | bytes 589832 | tf_op jit(solution)/shard_map/ppermute | solution.py:372
  56.3 3.5 %collective-permute-start.18 = (bf16[2,128,768]{2,1,0:T(8,128)(2,1)S(1)}, bf16[2,128,768]{2,1,0:T(8,128)(2,1)S(1)}, u32[]{:S(2)}, u32[]{:S(2)}) collective-permute-start(bf16[2,128,768]{2,1,0:T(8,128)(2,1)S(1)} %get-tuple-element.71), channel_id=1, source_target_pairs={{0,4},{4,0},{8,12},{12,8},{1,5},{5,1},{9,13},{13,9},{2,6},{6,2},{1... | collective-permute-start | bytes 1179656 | tf_op jit(solution)/shard_map/ppermute | solution.py:372
  59.7 3.6 %collective-permute-start.19 = (bf16[2,128,768]{2,1,0:T(8,128)(2,1)S(1)}, bf16[2,128,768]{2,1,0:T(8,128)(2,1)S(1)}, u32[]{:S(2)}, u32[]{:S(2)}) collective-permute-start(bf16[2,128,768]{2,1,0:T(8,128)(2,1)S(1)} %get-tuple-element.75), channel_id=1, source_target_pairs={{0,4},{4,0},{8,12},{12,8},{1,5},{5,1},{9,13},{13,9},{2,6},{6,2},{1... | collective-permute-start | bytes 1179656 | tf_op jit(solution)/shard_map/ppermute | solution.py:372
  62.8 4.8 %collective-permute-start.26 = (bf16[2,128,768]{2,1,0:T(8,128)(2,1)S(1)}, bf16[2,128,768]{2,1,0:T(8,128)(2,1)S(1)}, u32[]{:S(2)}, u32[]{:S(2)}) collective-permute-start(bf16[2,128,768]{2,1,0:T(8,128)(2,1)S(1)} %get-tuple-element.84), channel_id=1, source_target_pairs={{0,4},{4,0},{8,12},{12,8},{1,5},{5,1},{9,13},{13,9},{2,6},{6,2},{1... | collective-permute-start | bytes 1179656 | tf_op jit(solution)/shard_map/ppermute | solution.py:372
  65.4 14.8 %collective-permute-start.20 = (bf16[2,128,768]{2,1,0:T(8,128)(2,1)S(1)}, bf16[2,128,768]{2,1,0:T(8,128)(2,1)S(1)}, u32[]{:S(2)}, u32[]{:S(2)}) collective-permute-start(bf16[2,128,768]{2,1,0:T(8,128)(2,1)S(1)} %get-tuple-element.78), channel_id=1, source_target_pairs={{0,4},{4,0},{8,12},{12,8},{1,5},{5,1},{9,13},{13,9},{2,6},{6,2},{1... | collective-permute-start | bytes 1179656 | tf_op jit(solution)/shard_map/ppermute | solution.py:372
  65.5 7.8 %collective-permute-start.22 = (bf16[128,768]{1,0:T(8,128)(2,1)S(1)}, bf16[128,768]{1,0:T(8,128)(2,1)S(1)}, u32[]{:S(2)}, u32[]{:S(2)}) collective-permute-start(bf16[128,768]{1,0:T(8,128)(2,1)S(1)} %get-tuple-element.72.refs_5_), channel_id=1, source_target_pairs={{0,8},{4,12},{8,0},{12,4},{1,9},{5,13},{9,1},{13,5},{2,10},{6,14},... | collective-permute-start | bytes 589832 | tf_op jit(solution)/shard_map/ppermute | solution.py:375
  66.1 11.5 %collective-permute-start.24 = (bf16[128,768]{1,0:T(8,128)(2,1)S(1)}, bf16[128,768]{1,0:T(8,128)(2,1)S(1)}, u32[]{:S(2)}, u32[]{:S(2)}) collective-permute-start(bf16[128,768]{1,0:T(8,128)(2,1)S(1)} %get-tuple-element.76.refs_5_), channel_id=1, source_target_pairs={{0,8},{4,12},{8,0},{12,4},{1,9},{5,13},{9,1},{13,5},{2,10},{6,14},... | collective-permute-start | bytes 589832 | tf_op jit(solution)/shard_map/ppermute | solution.py:375
  67.7 13.5 %collective-permute-start.27 = (bf16[128,768]{1,0:T(8,128)(2,1)S(1)}, bf16[128,768]{1,0:T(8,128)(2,1)S(1)}, u32[]{:S(2)}, u32[]{:S(2)}) collective-permute-start(bf16[128,768]{1,0:T(8,128)(2,1)S(1)} %get-tuple-element.86), channel_id=1, source_target_pairs={{0,8},{4,12},{8,0},{12,4},{1,9},{5,13},{9,1},{13,5},{2,10},{6,14},... | collective-permute-start | bytes 589832 | tf_op jit(solution)/shard_map/ppermute | solution.py:375
  73.4 8.9 %collective-permute-start.23 = (bf16[128,768]{1,0:T(8,128)(2,1)S(1)}, bf16[128,768]{1,0:T(8,128)(2,1)S(1)}, u32[]{:S(2)}, u32[]{:S(2)}) collective-permute-start(bf16[128,768]{1,0:T(8,128)(2,1)S(1)} %shard_map.77), channel_id=1, source_target_pairs={{0,3},{1,2},{2,1},{3,0},{4,7},{5,6},{6,5},{7,4},{8,11},{9,10},{10,... | collective-permute-start | bytes 589832 | tf_op jit(solution)/shard_map/ppermute | solution.py:378
  77.6 15.2 %collective-permute-start.25 = (bf16[128,768]{1,0:T(8,128)(2,1)S(1)}, bf16[128,768]{1,0:T(8,128)(2,1)S(1)}, u32[]{:S(2)}, u32[]{:S(2)}) collective-permute-start(bf16[128,768]{1,0:T(8,128)(2,1)S(1)} %shard_map.78), channel_id=1, source_target_pairs={{0,2},{1,3},{2,0},{3,1},{4,6},{5,7},{6,4},{7,5},{8,10},{9,11},{10,... | collective-permute-start | bytes 589832 | tf_op jit(solution)/shard_map/ppermute | solution.py:378
  80.4 12.4 %collective-permute-start.21 = (bf16[128,768]{1,0:T(8,128)(2,1)S(1)}, bf16[128,768]{1,0:T(8,128)(2,1)S(1)}, u32[]{:S(2)}, u32[]{:S(2)}) collective-permute-start(bf16[128,768]{1,0:T(8,128)(2,1)S(1)} %get-tuple-element.80), channel_id=1, source_target_pairs={{0,8},{4,12},{8,0},{12,4},{1,9},{5,13},{9,1},{13,5},{2,10},{6,14},... | collective-permute-start | bytes 589832 | tf_op jit(solution)/shard_map/ppermute | solution.py:375
  81.3 11.5 %collective-permute-start.28 = (bf16[128,768]{1,0:T(8,128)(2,1)S(1)}, bf16[128,768]{1,0:T(8,128)(2,1)S(1)}, u32[]{:S(2)}, u32[]{:S(2)}) collective-permute-start(bf16[128,768]{1,0:T(8,128)(2,1)S(1)} %shard_map.80), channel_id=1, source_target_pairs={{0,1},{1,0},{2,3},{3,2},{4,5},{5,4},{6,7},{7,6},{8,9},{9,8},{10,11... | collective-permute-start | bytes 589832 | tf_op jit(solution)/shard_map/ppermute | solution.py:378

commit v3 on v2

--- a/solution.py
+++ b/solution.py
@@ -412,7 +412,7 @@
     planned = plan if kernels else plan_plain
     sel, back, sign = planned(table, names, experts, router_weight.shape[1])
 
-    down_order = [k for k in range(nh - 1, 0, -1)] + [0]
+    down_order = ([low, top] if nh >= 4 else []) + [k for k in range(nh - 1, 0, -1) if nh < 4 or k not in (low, top)] + [0]
     acc = None
     small = []
     for at, k in enumerate(order):
@@ -432,6 +432,7 @@
 
     total = []
     sent = []
+    passed = None
     for at, k in enumerate(down_order):
         if kernels:
             spot = None if at == nh - 1 else down_order[at + 1]
@@ -451,11 +452,16 @@
         if k == 0:
             total = [base] + [v.astype(f32) for v in parts] + total
             continue
+        if k == top and passed is not None:
+            parts.append(passed)
         if kernels:
             mid = chip_sum(base, parts, bf16)
         else:
             mid = sum([v.astype(f32) for v in parts], base).astype(bf16)
-        total.append(over_z(mid, k).astype(f32))
+        if k == low and nh >= 4:
+            passed = over_z(mid, 1)
+        else:
+            total.append(over_z(mid, k).astype(f32))
     total = functools.reduce(jnp.add, total)
     return total.astype(bf16)
 

time: 93.7 us -> 91.4 us (0.975)
  waiting for transfers between devices: 31.1 us -> 28.9 us
    ppermute x6, waiting for transfers between devices: 11 us -> 6.82 us  [over_z(): return lax.ppermute(v, 'hidden', [(i, i ^ k) for i in range(nh)])]
    ppermute x9, waiting for transfers between devices: 18.7 us -> 20.7 us  [over_x(): return lax.ppermute(v, 'expert', [(i, i ^ 2 * d) for i in range(blocks)])]
    ppermute x6, starting transfers between devices: 11.3 us -> 10.3 us  [over_z(): return lax.ppermute(v, 'hidden', [(i, i ^ k) for i in range(nh)])]
  transfers between devices with their start and end apart: 29 -> 29, of which waited for: 10 -> 11; matrix products, arithmetic and copies ran while one was open for 0% -> 0% of each run, Pallas kernels for 29% -> 30%
where the time goes in v3:
time: 91.4 us; the launch traced here: 91.3 us
  Pallas kernels  35.3 us (39%)
  waiting for transfers between devices  28.9 us (32%)
  starting transfers between devices  25.2 us (28%)
  local copies, waits for them, and re-layouts  0.93 us (1%)
    ppermute x9, waiting for transfers between devices, over_x(): return lax.ppermute(v, 'expert', [(i, i ^ 2 * d) for i in range(blocks)])  20.7 us
    pallas_call x4, Pallas kernels, up_chunk(): pl.pallas_call(functools.partial(up_kernel, first, last, blocks, experts)...  20.5 us
    ppermute x9, starting transfers between devices, over_x(): return lax.ppermute(v, 'expert', [(i, i ^ 2 * d) for i in range(blocks)])  12.8 us
    pallas_call x4, Pallas kernels, down_chunk(): pl.pallas_call(functools.partial(down_kernel, experts, blocks, last), out...  10.6 us
    ppermute x6, starting transfers between devices, over_z(): return lax.ppermute(v, 'hidden', [(i, i ^ k) for i in range(nh)])  10.3 us
    ppermute x6, waiting for transfers between devices, over_z(): return lax.ppermute(v, 'hidden', [(i, i ^ k) for i in range(nh)])  6.82 us
    pallas_call x1, Pallas kernels, first_fetch(): pl.pallas_call(functools.partial(first_kernel, len(table)), out_shape=(ja...  3.14 us
    ppermute x14, starting transfers between devices, over_core(): return lax.ppermute(v, 'expert', [(i, i ^ 1) for i in range(blocks)])  2.05 us
  transfers between devices with their start and end apart: 29, of which 11 were waited for; matrix products, arithmetic and copies ran while one was open for 0% of the time, Pallas kernels for 30%

profile of v3, /device:TPU:0, one launch (start us, length us, event | category | flops | bytes accessed | tf_op | source)
XLA Modules:
  0.0 91.3 jit_solution(4291418157903651010)
XLA Ops:
  0.0 3.0 %collective-permute-start.9 = (bf16[128,768]{1,0:T(8,128)(2,1)}, bf16[128,768]{1,0:T(8,128)(2,1)S(1)}, u32[]{:S(2)}, u32[]{:S(2)}) collective-permute-start(bf16[128,768]{1,0:T(8,128)(2,1)} %refs_5_.1), channel_id=1, source_target_pairs={{0,8},{4,12},{8,0},{12,4},{1,9},{5,13},{9,1},{13,5},{2,10},{6,14},... | collective-permute-start | bytes 589832 | tf_op jit(solution)/shard_map/ppermute | solution.py:375
  3.0 1.6 %collective-permute-start.14 = (bf16[128,768]{1,0:T(8,128)(2,1)}, bf16[128,768]{1,0:T(8,128)(2,1)S(1)}, u32[]{:S(2)}, u32[]{:S(2)}) collective-permute-start(bf16[128,768]{1,0:T(8,128)(2,1)} %refs_5_.1), channel_id=1, source_target_pairs={{0,1},{1,0},{2,3},{3,2},{4,5},{5,4},{6,7},{7,6},{8,9},{9,8},{10,11... | collective-permute-start | bytes 589832 | tf_op jit(solution)/shard_map/ppermute | solution.py:378
  4.5 2.5 %collective-permute-start = (bf16[128,768]{1,0:T(8,128)(2,1)}, bf16[128,768]{1,0:T(8,128)(2,1)S(1)}, u32[]{:S(2)}, u32[]{:S(2)}) collective-permute-start(bf16[128,768]{1,0:T(8,128)(2,1)} %refs_5_.1), channel_id=1, source_target_pairs={{0,3},{1,2},{2,1},{3,0},{4,7},{5,6},{6,5},{7,4},{8,11},{9,10},{10,... | collective-permute-start | bytes 589832 | tf_op jit(solution)/shard_map/ppermute | solution.py:378
  7.0 1.1 %collective-permute-done.9.refs_4_ = bf16[128,768]{1,0:T(8,128)(2,1)S(1)} collective-permute-done((bf16[128,768]{1,0:T(8,128)(2,1)}, bf16[128,768]{1,0:T(8,128)(2,1)S(1)}, u32[]{:S(2)}, u32[]{:S(2)}) %collective-permute-start.9) | collective-permute-done | bytes 196640 | tf_op jit(solution)/shard_map/ppermute | solution.py:375
  8.1 1.7 %collective-permute-start.6 = (s32[2,128]{1,0:T(2,128)}, s32[2,128]{1,0:T(2,128)S(1)}, u32[]{:S(2)}, u32[]{:S(2)}) collective-permute-start(s32[2,128]{1,0:T(2,128)} %bitcast.7), channel_id=1, source_target_pairs={{0,8},{4,12},{8,0},{12,4},{1,9},{5,13},{9,1},{13,5},{2,10},{6,14},... | collective-permute-start | bytes 3080 | tf_op jit(solution)/shard_map/ppermute | solution.py:375
  9.8 2.0 %collective-permute-done.6.refs_2_ = s32[2,128]{1,0:T(2,128)S(1)} collective-permute-done((s32[2,128]{1,0:T(2,128)}, s32[2,128]{1,0:T(2,128)S(1)}, u32[]{:S(2)}, u32[]{:S(2)}) %collective-permute-start.6) | collective-permute-done | bytes 1056 | tf_op jit(solution)/shard_map/ppermute | solution.py:375
  11.9 1.4 %collective-permute-done.5.refs_1_ = s32[2,128]{1,0:T(2,128)S(1)} collective-permute-done((s32[2,128]{1,0:T(2,128)}, s32[2,128]{1,0:T(2,128)S(1)}, u32[]{:S(2)}, u32[]{:S(2)}) %collective-permute-start.5) | collective-permute-done | bytes 1056 | tf_op jit(solution)/shard_map/ppermute | solution.py:372
  13.4 0.9 %copy-done = bf16[128,768]{1,0:T(8,128)(2,1)S(1)} copy-done((bf16[128,768]{1,0:T(8,128)(2,1)S(1)}, bf16[128,768]{1,0:T(8,128)(2,1)}, u32[]{:S(2)}) %copy-start) | copy-done | bytes 196632
  14.3 3.1 %shard_map.65 = (bf16[128,768]{1,0:T(8,128)(2,1)S(1)}, bf16[8,3072]{1,0:T(8,128)(2,1)S(1)}, bf16[2,768,2048]{2,1,0:T(8,128)(2,1)S(1)}) custom-call(s32[1]{0:T(128)} %bitcast.refs_0_, s32[1]{0:T(128)} %bitcast.4.refs_1_.refs_0_, s32[1]{0:T(128)} %bitcast.1.refs_2_.refs_1_.refs_0_, s32[1]{0:T(128)} %bitcast.5.refs_3_.refs_1_.refs_0_, s32[1]{0:T(128)} %bitcast.2.base.refs_4_, ...), custom_call_target="tpu_custom_call" | custom-call | bytes 6291456 | tf_op jit(solution)/shard_map/pallas_call | solution.py:112
  18.0 1.8 %collective-permute-start.16 = (bf16[128,768]{1,0:T(8,128)(2,1)S(1)}, bf16[128,768]{1,0:T(8,128)(2,1)S(1)}, u32[]{:S(2)}, u32[]{:S(2)}) collective-permute-start(bf16[128,768]{1,0:T(8,128)(2,1)S(1)} %collective-permute-done.14.refs_2_), channel_id=1, source_target_pairs={{0,8},{4,12},{8,0},{12,4},{1,9},{5,13},{9,1},{13,5},{2,10},{6,14},... | collective-permute-start | bytes 589832 | tf_op jit(solution)/shard_map/ppermute | solution.py:375
  19.9 1.6 %collective-permute-start.1 = (bf16[128,768]{1,0:T(8,128)(2,1)S(1)}, bf16[128,768]{1,0:T(8,128)(2,1)S(1)}, u32[]{:S(2)}, u32[]{:S(2)}) collective-permute-start(bf16[128,768]{1,0:T(8,128)(2,1)S(1)} %collective-permute-done.refs_2_), channel_id=1, source_target_pairs={{0,1},{1,0},{2,3},{3,2},{4,5},{5,4},{6,7},{7,6},{8,9},{9,8},{10,11... | collective-permute-start | bytes 589832 | tf_op jit(solution)/shard_map/ppermute | solution.py:378
  21.5 5.1 %shard_map.66 = (f32[2,192,2048]{2,1,0:T(8,128)S(1)}, f32[2,192,2048]{2,1,0:T(8,128)S(1)}, f32[4,8,128]{2,1,0:T(8,128)S(1)}, bf16[2,768,2048]{2,1,0:T(8,128)(2,1)S(1)}) custom-call(s32[1]{0:T(128)} %bitcast.refs_0_, s32[1]{0:T(128)} %bitcast.4.refs_1_.refs_0_, bf16[128,768]{1,0:T(8,128)(2,1)S(1)} %get-tuple-element.48.refs_2_, ...), custom_call_target="tpu_custom_call" | custom-call | flops 2415919104 | bytes 12582912 | tf_op jit(solution)/shard_map/pallas_call | solution.py:218
  27.2 1.5 %collective-permute-start.3 = (bf16[128,768]{1,0:T(8,128)(2,1)S(1)}, bf16[128,768]{1,0:T(8,128)(2,1)S(1)}, u32[]{:S(2)}, u32[]{:S(2)}) collective-permute-start(bf16[128,768]{1,0:T(8,128)(2,1)S(1)} %collective-permute-done.1.refs_2_), channel_id=1, source_target_pairs={{0,8},{4,12},{8,0},{12,4},{1,9},{5,13},{9,1},{13,5},{2,10},{6,14},... | collective-permute-start | bytes 589832 | tf_op jit(solution)/shard_map/ppermute | solution.py:375
  29.2 5.2 %collective-permute-done.12.refs_4_ = bf16[128,768]{1,0:T(8,128)(2,1)S(1)} collective-permute-done((bf16[128,768]{1,0:T(8,128)(2,1)S(1)}, bf16[128,768]{1,0:T(8,128)(2,1)S(1)}, u32[]{:S(2)}, u32[]{:S(2)}) %collective-permute-start.12) | collective-permute-done | bytes 196640 | tf_op jit(solution)/shard_map/ppermute | solution.py:375
  34.4 3.4 %collective-permute-done.3.refs_4_ = bf16[128,768]{1,0:T(8,128)(2,1)S(1)} collective-permute-done((bf16[128,768]{1,0:T(8,128)(2,1)S(1)}, bf16[128,768]{1,0:T(8,128)(2,1)S(1)}, u32[]{:S(2)}, u32[]{:S(2)}) %collective-permute-start.3) | collective-permute-done | bytes 196640 | tf_op jit(solution)/shard_map/ppermute | solution.py:375
  37.8 5.0 %shard_map.67 = (f32[2,192,2048]{2,1,0:T(8,128)S(1)}, f32[2,192,2048]{2,1,0:T(8,128)S(1)}, f32[4,8,128]{2,1,0:T(8,128)S(1)}, bf16[2,768,2048]{2,1,0:T(8,128)(2,1)S(1)}) custom-call(s32[1]{0:T(128)} %bitcast.4.refs_1_.refs_0_, s32[1]{0:T(128)} %bitcast.5.refs_3_.refs_1_.refs_0_, ...), custom_call_target="tpu_custom_call", output_to_operand_aliasing={{0}: (11, {}), {1}: (12, {}), {2}: (13, {})} | custom-call | flops 2415919104 | bytes 12582912 | tf_op jit(solution)/shard_map/pallas_call | solution.py:218
  42.9 5.0 %shard_map.68 = (f32[2,192,2048]{2,1,0:T(8,128)S(1)}, f32[2,192,2048]{2,1,0:T(8,128)S(1)}, f32[4,8,128]{2,1,0:T(8,128)S(1)}, bf16[2,768,2048]{2,1,0:T(8,128)(2,1)S(1)}) custom-call(s32[1]{0:T(128)} %bitcast.5.refs_3_.refs_1_.refs_0_, s32[1]{0:T(128)} %bitcast.1.refs_2_.refs_1_.refs_0_, ...), custom_call_target="tpu_custom_call", output_to_operand_aliasing={{0}: (11, {}), {1}: (12, {}), {2}: (13, {})} | custom-call | flops 2415919104 | bytes 12582912 | tf_op jit(solution)/shard_map/pallas_call | solution.py:218
  47.9 5.4 %shard_map.69 = (bf16[2,192,2048]{2,1,0:T(8,128)(2,1)S(1)}, f32[2,192,1]{2,1,0:T(8,128)S(1)}, bf16[2,2048,768]{2,1,0:T(8,128)(2,1)S(1)}) custom-call(s32[1]{0:T(128)} %bitcast.1.refs_2_.refs_1_.refs_0_, s32[1]{0:T(128)} %bitcast.1.refs_2_.refs_1_.refs_0_, bf16[128,768]{1,0:T(8,128)(2,1)S(1)} %collective-permute-done.1.refs_2_, ...), custom_call_target="tpu_custom_call" | custom-call | flops 2415919104 | bytes 12582912 | tf_op jit(solution)/shard_map/pallas_call | solution.py:218
  53.3 2.9 %shard_map.70 = (bf16[2,128,768]{2,1,0:T(8,128)(2,1)S(1)}, bf16[2,128,768]{2,1,0:T(8,128)(2,1)S(1)}, bf16[2,2048,768]{2,1,0:T(8,128)(2,1)S(1)}) custom-call(s32[1]{0:T(128)} %bitcast.5.refs_3_.refs_1_.refs_0_, bf16[2,192,2048]{2,1,0:T(8,128)(2,1)S(1)} %get-tuple-element.64.refs_1_, bf16[4,128,96]{2,1,0:T(8,128)(2,1)S(1)} %get-tuple-element.65.refs_2_, ...), custom_call_target="tpu_custom_call" | custom-call | flops 1207959552 | bytes 6291456 | tf_op jit(solution)/shard_map/pallas_call | solution.py:295
  56.8 2.9 %shard_map.71 = (bf16[2,128,768]{2,1,0:T(8,128)(2,1)S(1)}, bf16[2,128,768]{2,1,0:T(8,128)(2,1)S(1)}, bf16[2,2048,768]{2,1,0:T(8,128)(2,1)S(1)}) custom-call(s32[1]{0:T(128)} %bitcast.4.refs_1_.refs_0_, bf16[2,192,2048]{2,1,0:T(8,128)(2,1)S(1)} %get-tuple-element.64.refs_1_, bf16[4,128,96]{2,1,0:T(8,128)(2,1)S(1)} %get-tuple-element.65.refs_2_, ...), custom_call_target="tpu_custom_call" | custom-call | flops 1207959552 | bytes 6291456 | tf_op jit(solution)/shard_map/pallas_call | solution.py:295
  59.9 2.9 %shard_map.73 = (bf16[2,128,768]{2,1,0:T(8,128)(2,1)S(1)}, bf16[2,128,768]{2,1,0:T(8,128)(2,1)S(1)}, bf16[2,2048,768]{2,1,0:T(8,128)(2,1)S(1)}) custom-call(s32[1]{0:T(128)} %bitcast.refs_0_, bf16[2,192,2048]{2,1,0:T(8,128)(2,1)S(1)} %get-tuple-element.64.refs_1_, bf16[4,128,96]{2,1,0:T(8,128)(2,1)S(1)} %get-tuple-element.65.refs_2_, ...), custom_call_target="tpu_custom_call" | custom-call | flops 1207959552 | bytes 6291456 | tf_op jit(solution)/shard_map/pallas_call | solution.py:295
  63.4 2.0 %shard_map.75 = (bf16[2,128,768]{2,1,0:T(8,128)(2,1)S(1)}, bf16[2,128,768]{2,1,0:T(8,128)(2,1)S(1)}) custom-call(s32[1]{0:T(128)} %bitcast.refs_0_, bf16[2,192,2048]{2,1,0:T(8,128)(2,1)S(1)} %get-tuple-element.64.refs_1_, bf16[4,128,96]{2,1,0:T(8,128)(2,1)S(1)} %get-tuple-element.65.refs_2_, f32[2,192,1]{2,1,0:T(8,128)S(1)} %get-tuple-element.66.refs_3_.refs_5_, ...), custom_call_target="tpu_custom_call" | custom-call | flops 1207959552 | bytes 6291456 | tf_op jit(solution)/shard_map/pallas_call | solution.py:295
  66.1 1.5 %collective-permute-start.22 = (bf16[128,768]{1,0:T(8,128)(2,1)S(1)}, bf16[128,768]{1,0:T(8,128)(2,1)S(1)}, u32[]{:S(2)}, u32[]{:S(2)}) collective-permute-start(bf16[128,768]{1,0:T(8,128)(2,1)S(1)} %get-tuple-element.76.refs_5_), channel_id=1, source_target_pairs={{0,8},{4,12},{8,0},{12,4},{1,9},{5,13},{9,1},{13,5},{2,10},{6,14},... | collective-permute-start | bytes 589832 | tf_op jit(solution)/shard_map/ppermute | solution.py:375
  67.6 5.7 %collective-permute-done.23.refs_0_ = bf16[128,768]{1,0:T(8,128)(2,1)S(1)} collective-permute-done((bf16[128,768]{1,0:T(8,128)(2,1)S(1)}, bf16[128,768]{1,0:T(8,128)(2,1)S(1)}, u32[]{:S(2)}, u32[]{:S(2)}) %collective-permute-start.23) | collective-permute-done | bytes 196640 | tf_op jit(solution)/shard_map/ppermute | solution.py:375
  74.5 1.7 %collective-permute-start.21 = (bf16[128,768]{1,0:T(8,128)(2,1)S(1)}, bf16[128,768]{1,0:T(8,128)(2,1)S(1)}, u32[]{:S(2)}, u32[]{:S(2)}) collective-permute-start(bf16[128,768]{1,0:T(8,128)(2,1)S(1)} %get-tuple-element.80), channel_id=1, source_target_pairs={{0,8},{4,12},{8,0},{12,4},{1,9},{5,13},{9,1},{13,5},{2,10},{6,14},... | collective-permute-start | bytes 589832 | tf_op jit(solution)/shard_map/ppermute | solution.py:375
  76.2 1.3 %collective-permute-done.22.refs_0_ = bf16[128,768]{1,0:T(8,128)(2,1)S(1)} collective-permute-done((bf16[128,768]{1,0:T(8,128)(2,1)S(1)}, bf16[128,768]{1,0:T(8,128)(2,1)S(1)}, u32[]{:S(2)}, u32[]{:S(2)}) %collective-permute-start.22) | collective-permute-done | bytes 196640 | tf_op jit(solution)/shard_map/ppermute | solution.py:375
  77.5 1.7 %collective-permute-done.24.refs_1_ = bf16[128,768]{1,0:T(8,128)(2,1)S(1)} collective-permute-done((bf16[128,768]{1,0:T(8,128)(2,1)S(1)}, bf16[128,768]{1,0:T(8,128)(2,1)S(1)}, u32[]{:S(2)}, u32[]{:S(2)}) %collective-permute-start.24) | collective-permute-done | bytes 196640 | tf_op jit(solution)/shard_map/ppermute | solution.py:378
  79.3 2.5 %collective-permute-start.25 = (bf16[128,768]{1,0:T(8,128)(2,1)S(1)}, bf16[128,768]{1,0:T(8,128)(2,1)S(1)}, u32[]{:S(2)}, u32[]{:S(2)}) collective-permute-start(bf16[128,768]{1,0:T(8,128)(2,1)S(1)} %shard_map.78), channel_id=1, source_target_pairs={{0,3},{1,2},{2,1},{3,0},{4,7},{5,6},{6,5},{7,4},{8,11},{9,10},{10,... | collective-permute-start | bytes 589832 | tf_op jit(solution)/shard_map/ppermute | solution.py:378
  81.9 1.6 %collective-permute-start.28 = (bf16[128,768]{1,0:T(8,128)(2,1)S(1)}, bf16[128,768]{1,0:T(8,128)(2,1)S(1)}, u32[]{:S(2)}, u32[]{:S(2)}) collective-permute-start(bf16[128,768]{1,0:T(8,128)(2,1)S(1)} %shard_map.80), channel_id=1, source_target_pairs={{0,1},{1,0},{2,3},{3,2},{4,5},{5,4},{6,7},{7,6},{8,9},{9,8},{10,11... | collective-permute-start | bytes 589832 | tf_op jit(solution)/shard_map/ppermute | solution.py:378
  83.5 1.9 %collective-permute-done.21 = bf16[128,768]{1,0:T(8,128)(2,1)S(1)} collective-permute-done((bf16[128,768]{1,0:T(8,128)(2,1)S(1)}, bf16[128,768]{1,0:T(8,128)(2,1)S(1)}, u32[]{:S(2)}, u32[]{:S(2)}) %collective-permute-start.21) | collective-permute-done | bytes 196640 | tf_op jit(solution)/shard_map/ppermute | solution.py:375
  85.4 2.9 %collective-permute-done.25 = bf16[128,768]{1,0:T(8,128)(2,1)S(1)} collective-permute-done((bf16[128,768]{1,0:T(8,128)(2,1)S(1)}, bf16[128,768]{1,0:T(8,128)(2,1)S(1)}, u32[]{:S(2)}, u32[]{:S(2)}) %collective-permute-start.25) | collective-permute-done | bytes 196640 | tf_op jit(solution)/shard_map/ppermute | solution.py:378
  88.3 2.2 %collective-permute-done.28 = bf16[128,768]{1,0:T(8,128)(2,1)S(1)} collective-permute-done((bf16[128,768]{1,0:T(8,128)(2,1)S(1)}, bf16[128,768]{1,0:T(8,128)(2,1)S(1)}, u32[]{:S(2)}, u32[]{:S(2)}) %collective-permute-start.28) | collective-permute-done | bytes 196640 | tf_op jit(solution)/shard_map/ppermute | solution.py:378
  (48 shorter events, 6.0 us)
Async XLA Ops:
  0.0 8.1 %collective-permute-start.9 = (bf16[128,768]{1,0:T(8,128)(2,1)}, bf16[128,768]{1,0:T(8,128)(2,1)S(1)}, u32[]{:S(2)}, u32[]{:S(2)}) collective-permute-start(bf16[128,768]{1,0:T(8,128)(2,1)} %refs_5_.1), channel_id=1, source_target_pairs={{0,8},{4,12},{8,0},{12,4},{1,9},{5,13},{9,1},{13,5},{2,10},{6,14},... | collective-permute-start | bytes 589832 | tf_op jit(solution)/shard_map/ppermute | solution.py:375
  3.0 15.1 %collective-permute-start.14 = (bf16[128,768]{1,0:T(8,128)(2,1)}, bf16[128,768]{1,0:T(8,128)(2,1)S(1)}, u32[]{:S(2)}, u32[]{:S(2)}) collective-permute-start(bf16[128,768]{1,0:T(8,128)(2,1)} %refs_5_.1), channel_id=1, source_target_pairs={{0,1},{1,0},{2,3},{3,2},{4,5},{5,4},{6,7},{7,6},{8,9},{9,8},{10,11... | collective-permute-start | bytes 589832 | tf_op jit(solution)/shard_map/ppermute | solution.py:378
  4.5 15.4 %collective-permute-start = (bf16[128,768]{1,0:T(8,128)(2,1)}, bf16[128,768]{1,0:T(8,128)(2,1)S(1)}, u32[]{:S(2)}, u32[]{:S(2)}) collective-permute-start(bf16[128,768]{1,0:T(8,128)(2,1)} %refs_5_.1), channel_id=1, source_target_pairs={{0,3},{1,2},{2,1},{3,0},{4,7},{5,6},{6,5},{7,4},{8,11},{9,10},{10,... | collective-permute-start | bytes 589832 | tf_op jit(solution)/shard_map/ppermute | solution.py:378
  7.0 14.5 %collective-permute-start.8 = (bf16[128,768]{1,0:T(8,128)(2,1)}, bf16[128,768]{1,0:T(8,128)(2,1)S(1)}, u32[]{:S(2)}, u32[]{:S(2)}) collective-permute-start(bf16[128,768]{1,0:T(8,128)(2,1)} %refs_5_.1), channel_id=1, source_target_pairs={{0,4},{4,0},{8,12},{12,8},{1,5},{5,1},{9,13},{13,9},{2,6},{6,2},{1... | collective-permute-start | bytes 589832 | tf_op jit(solution)/shard_map/ppermute | solution.py:372
  8.1 13.4 %collective-permute-start.10 = (bf16[128,768]{1,0:T(8,128)(2,1)S(1)}, bf16[128,768]{1,0:T(8,128)(2,1)S(1)}, u32[]{:S(2)}, u32[]{:S(2)}) collective-permute-start(bf16[128,768]{1,0:T(8,128)(2,1)S(1)} %collective-permute-done.9.refs_4_), channel_id=1, source_target_pairs={{0,4},{4,0},{8,12},{12,8},{1,5},{5,1},{9,13},{13,9},{2,6},{6,2},{1... | collective-permute-start | bytes 589832 | tf_op jit(solution)/shard_map/ppermute | solution.py:372
  8.1 3.8 %collective-permute-start.6 = (s32[2,128]{1,0:T(2,128)}, s32[2,128]{1,0:T(2,128)S(1)}, u32[]{:S(2)}, u32[]{:S(2)}) collective-permute-start(s32[2,128]{1,0:T(2,128)} %bitcast.7), channel_id=1, source_target_pairs={{0,8},{4,12},{8,0},{12,4},{1,9},{5,13},{9,1},{13,5},{2,10},{6,14},... | collective-permute-start | bytes 3080 | tf_op jit(solution)/shard_map/ppermute | solution.py:375
  11.9 1.4 %collective-permute-start.5 = (s32[2,128]{1,0:T(2,128)}, s32[2,128]{1,0:T(2,128)S(1)}, u32[]{:S(2)}, u32[]{:S(2)}) collective-permute-start(s32[2,128]{1,0:T(2,128)} %bitcast.8), channel_id=1, source_target_pairs={{0,4},{4,0},{8,12},{12,8},{1,5},{5,1},{9,13},{13,9},{2,6},{6,2},{1... | collective-permute-start | bytes 3080 | tf_op jit(solution)/shard_map/ppermute | solution.py:372
  13.2 4.3 %collective-permute-start.7 = (s32[2,128]{1,0:T(2,128)S(1)}, s32[2,128]{1,0:T(2,128)S(1)}, u32[]{:S(2)}, u32[]{:S(2)}) collective-permute-start(s32[2,128]{1,0:T(2,128)S(1)} %collective-permute-done.6.refs_2_), channel_id=1, source_target_pairs={{0,4},{4,0},{8,12},{12,8},{1,5},{5,1},{9,13},{13,9},{2,6},{6,2},{1... | collective-permute-start | bytes 3080 | tf_op jit(solution)/shard_map/ppermute | solution.py:372
  13.4 0.9 %copy-start = (bf16[128,768]{1,0:T(8,128)(2,1)S(1)}, bf16[128,768]{1,0:T(8,128)(2,1)}, u32[]{:S(2)}) copy-start(bf16[128,768]{1,0:T(8,128)(2,1)} %refs_5_.1) | copy-start | bytes 589828
  14.3 3.2 %copy-start.1 = (s32[128,2]{0,1:T(2,128)S(1)}, s32[128,2]{0,1:T(2,128)}, u32[]{:S(2)}) copy-start(s32[128,2]{0,1:T(2,128)} %param.7) | copy-start | bytes 3076
  18.0 10.6 %collective-permute-start.16 = (bf16[128,768]{1,0:T(8,128)(2,1)S(1)}, bf16[128,768]{1,0:T(8,128)(2,1)S(1)}, u32[]{:S(2)}, u32[]{:S(2)}) collective-permute-start(bf16[128,768]{1,0:T(8,128)(2,1)S(1)} %collective-permute-done.14.refs_2_), channel_id=1, source_target_pairs={{0,8},{4,12},{8,0},{12,4},{1,9},{5,13},{9,1},{13,5},{2,10},{6,14},... | collective-permute-start | bytes 589832 | tf_op jit(solution)/shard_map/ppermute | solution.py:375
  19.8 9.3 %collective-permute-start.15 = (bf16[128,768]{1,0:T(8,128)(2,1)S(1)}, bf16[128,768]{1,0:T(8,128)(2,1)S(1)}, u32[]{:S(2)}, u32[]{:S(2)}) collective-permute-start(bf16[128,768]{1,0:T(8,128)(2,1)S(1)} %collective-permute-done.14.refs_2_), channel_id=1, source_target_pairs={{0,4},{4,0},{8,12},{12,8},{1,5},{5,1},{9,13},{13,9},{2,6},{6,2},{1... | collective-permute-start | bytes 589832 | tf_op jit(solution)/shard_map/ppermute | solution.py:372
  19.9 7.3 %collective-permute-start.1 = (bf16[128,768]{1,0:T(8,128)(2,1)S(1)}, bf16[128,768]{1,0:T(8,128)(2,1)S(1)}, u32[]{:S(2)}, u32[]{:S(2)}) collective-permute-start(bf16[128,768]{1,0:T(8,128)(2,1)S(1)} %collective-permute-done.refs_2_), channel_id=1, source_target_pairs={{0,1},{1,0},{2,3},{3,2},{4,5},{5,4},{6,7},{7,6},{8,9},{9,8},{10,11... | collective-permute-start | bytes 589832 | tf_op jit(solution)/shard_map/ppermute | solution.py:378
  26.6 7.8 %collective-permute-start.12 = (bf16[128,768]{1,0:T(8,128)(2,1)S(1)}, bf16[128,768]{1,0:T(8,128)(2,1)S(1)}, u32[]{:S(2)}, u32[]{:S(2)}) collective-permute-start(bf16[128,768]{1,0:T(8,128)(2,1)S(1)} %collective-permute-done.refs_2_), channel_id=1, source_target_pairs={{0,8},{4,12},{8,0},{12,4},{1,9},{5,13},{9,1},{13,5},{2,10},{6,14},... | collective-permute-start | bytes 589832 | tf_op jit(solution)/shard_map/ppermute | solution.py:375
  27.2 10.7 %collective-permute-start.3 = (bf16[128,768]{1,0:T(8,128)(2,1)S(1)}, bf16[128,768]{1,0:T(8,128)(2,1)S(1)}, u32[]{:S(2)}, u32[]{:S(2)}) collective-permute-start(bf16[128,768]{1,0:T(8,128)(2,1)S(1)} %collective-permute-done.1.refs_2_), channel_id=1, source_target_pairs={{0,8},{4,12},{8,0},{12,4},{1,9},{5,13},{9,1},{13,5},{2,10},{6,14},... | collective-permute-start | bytes 589832 | tf_op jit(solution)/shard_map/ppermute | solution.py:375
  28.7 9.2 %collective-permute-start.17 = (bf16[128,768]{1,0:T(8,128)(2,1)S(1)}, bf16[128,768]{1,0:T(8,128)(2,1)S(1)}, u32[]{:S(2)}, u32[]{:S(2)}) collective-permute-start(bf16[128,768]{1,0:T(8,128)(2,1)S(1)} %collective-permute-done.16.refs_4_), channel_id=1, source_target_pairs={{0,4},{4,0},{8,12},{12,8},{1,5},{5,1},{9,13},{13,9},{2,6},{6,2},{1... | collective-permute-start | bytes 589832 | tf_op jit(solution)/shard_map/ppermute | solution.py:372
  28.7 14.2 %collective-permute-start.11 = (bf16[128,768]{1,0:T(8,128)(2,1)S(1)}, bf16[128,768]{1,0:T(8,128)(2,1)S(1)}, u32[]{:S(2)}, u32[]{:S(2)}) collective-permute-start(bf16[128,768]{1,0:T(8,128)(2,1)S(1)} %collective-permute-done.refs_2_), channel_id=1, source_target_pairs={{0,4},{4,0},{8,12},{12,8},{1,5},{5,1},{9,13},{13,9},{2,6},{6,2},{1... | collective-permute-start | bytes 589832 | tf_op jit(solution)/shard_map/ppermute | solution.py:372
  29.2 18.7 %collective-permute-start.2 = (bf16[128,768]{1,0:T(8,128)(2,1)S(1)}, bf16[128,768]{1,0:T(8,128)(2,1)S(1)}, u32[]{:S(2)}, u32[]{:S(2)}) collective-permute-start(bf16[128,768]{1,0:T(8,128)(2,1)S(1)} %collective-permute-done.1.refs_2_), channel_id=1, source_target_pairs={{0,4},{4,0},{8,12},{12,8},{1,5},{5,1},{9,13},{13,9},{2,6},{6,2},{1... | collective-permute-start | bytes 589832 | tf_op jit(solution)/shard_map/ppermute | solution.py:372
  34.4 8.5 %collective-permute-start.13 = (bf16[128,768]{1,0:T(8,128)(2,1)S(1)}, bf16[128,768]{1,0:T(8,128)(2,1)S(1)}, u32[]{:S(2)}, u32[]{:S(2)}) collective-permute-start(bf16[128,768]{1,0:T(8,128)(2,1)S(1)} %collective-permute-done.12.refs_4_), channel_id=1, source_target_pairs={{0,4},{4,0},{8,12},{12,8},{1,5},{5,1},{9,13},{13,9},{2,6},{6,2},{1... | collective-permute-start | bytes 589832 | tf_op jit(solution)/shard_map/ppermute | solution.py:372
  37.8 10.1 %collective-permute-start.4 = (bf16[128,768]{1,0:T(8,128)(2,1)S(1)}, bf16[128,768]{1,0:T(8,128)(2,1)S(1)}, u32[]{:S(2)}, u32[]{:S(2)}) collective-permute-start(bf16[128,768]{1,0:T(8,128)(2,1)S(1)} %collective-permute-done.3.refs_4_), channel_id=1, source_target_pairs={{0,4},{4,0},{8,12},{12,8},{1,5},{5,1},{9,13},{13,9},{2,6},{6,2},{1... | collective-permute-start | bytes 589832 | tf_op jit(solution)/shard_map/ppermute | solution.py:372
  56.2 3.6 %collective-permute-start.18 = (bf16[2,128,768]{2,1,0:T(8,128)(2,1)S(1)}, bf16[2,128,768]{2,1,0:T(8,128)(2,1)S(1)}, u32[]{:S(2)}, u32[]{:S(2)}) collective-permute-start(bf16[2,128,768]{2,1,0:T(8,128)(2,1)S(1)} %get-tuple-element.71), channel_id=1, source_target_pairs={{0,4},{4,0},{8,12},{12,8},{1,5},{5,1},{9,13},{13,9},{2,6},{6,2},{1... | collective-permute-start | bytes 1179656 | tf_op jit(solution)/shard_map/ppermute | solution.py:372
  59.7 3.6 %collective-permute-start.19 = (bf16[2,128,768]{2,1,0:T(8,128)(2,1)S(1)}, bf16[2,128,768]{2,1,0:T(8,128)(2,1)S(1)}, u32[]{:S(2)}, u32[]{:S(2)}) collective-permute-start(bf16[2,128,768]{2,1,0:T(8,128)(2,1)S(1)} %get-tuple-element.75), channel_id=1, source_target_pairs={{0,4},{4,0},{8,12},{12,8},{1,5},{5,1},{9,13},{13,9},{2,6},{6,2},{1... | collective-permute-start | bytes 1179656 | tf_op jit(solution)/shard_map/ppermute | solution.py:372
  62.8 11.1 %collective-permute-start.26 = (bf16[2,128,768]{2,1,0:T(8,128)(2,1)S(1)}, bf16[2,128,768]{2,1,0:T(8,128)(2,1)S(1)}, u32[]{:S(2)}, u32[]{:S(2)}) collective-permute-start(bf16[2,128,768]{2,1,0:T(8,128)(2,1)S(1)} %get-tuple-element.84), channel_id=1, source_target_pairs={{0,4},{4,0},{8,12},{12,8},{1,5},{5,1},{9,13},{13,9},{2,6},{6,2},{1... | collective-permute-start | bytes 1179656 | tf_op jit(solution)/shard_map/ppermute | solution.py:372
  65.4 9.0 %collective-permute-start.20 = (bf16[2,128,768]{2,1,0:T(8,128)(2,1)S(1)}, bf16[2,128,768]{2,1,0:T(8,128)(2,1)S(1)}, u32[]{:S(2)}, u32[]{:S(2)}) collective-permute-start(bf16[2,128,768]{2,1,0:T(8,128)(2,1)S(1)} %get-tuple-element.78), channel_id=1, source_target_pairs={{0,4},{4,0},{8,12},{12,8},{1,5},{5,1},{9,13},{13,9},{2,6},{6,2},{1... | collective-permute-start | bytes 1179656 | tf_op jit(solution)/shard_map/ppermute | solution.py:372
  65.5 7.8 %collective-permute-start.23 = (bf16[128,768]{1,0:T(8,128)(2,1)S(1)}, bf16[128,768]{1,0:T(8,128)(2,1)S(1)}, u32[]{:S(2)}, u32[]{:S(2)}) collective-permute-start(bf16[128,768]{1,0:T(8,128)(2,1)S(1)} %get-tuple-element.72.refs_5_), channel_id=1, source_target_pairs={{0,8},{4,12},{8,0},{12,4},{1,9},{5,13},{9,1},{13,5},{2,10},{6,14},... | collective-permute-start | bytes 589832 | tf_op jit(solution)/shard_map/ppermute | solution.py:375
  66.1 11.5 %collective-permute-start.22 = (bf16[128,768]{1,0:T(8,128)(2,1)S(1)}, bf16[128,768]{1,0:T(8,128)(2,1)S(1)}, u32[]{:S(2)}, u32[]{:S(2)}) collective-permute-start(bf16[128,768]{1,0:T(8,128)(2,1)S(1)} %get-tuple-element.76.refs_5_), channel_id=1, source_target_pairs={{0,8},{4,12},{8,0},{12,4},{1,9},{5,13},{9,1},{13,5},{2,10},{6,14},... | collective-permute-start | bytes 589832 | tf_op jit(solution)/shard_map/ppermute | solution.py:375
  73.4 5.9 %collective-permute-start.24 = (bf16[128,768]{1,0:T(8,128)(2,1)S(1)}, bf16[128,768]{1,0:T(8,128)(2,1)S(1)}, u32[]{:S(2)}, u32[]{:S(2)}) collective-permute-start(bf16[128,768]{1,0:T(8,128)(2,1)S(1)} %shard_map.77), channel_id=1, source_target_pairs={{0,1},{1,0},{2,3},{3,2},{4,5},{5,4},{6,7},{7,6},{8,9},{9,8},{10,11... | collective-permute-start | bytes 589832 | tf_op jit(solution)/shard_map/ppermute | solution.py:378
  74.0 7.9 %collective-permute-start.27 = (bf16[128,768]{1,0:T(8,128)(2,1)S(1)}, bf16[128,768]{1,0:T(8,128)(2,1)S(1)}, u32[]{:S(2)}, u32[]{:S(2)}) collective-permute-start(bf16[128,768]{1,0:T(8,128)(2,1)S(1)} %get-tuple-element.86), channel_id=1, source_target_pairs={{0,8},{4,12},{8,0},{12,4},{1,9},{5,13},{9,1},{13,5},{2,10},{6,14},... | collective-permute-start | bytes 589832 | tf_op jit(solution)/shard_map/ppermute | solution.py:375
  74.5 10.9 %collective-permute-start.21 = (bf16[128,768]{1,0:T(8,128)(2,1)S(1)}, bf16[128,768]{1,0:T(8,128)(2,1)S(1)}, u32[]{:S(2)}, u32[]{:S(2)}) collective-permute-start(bf16[128,768]{1,0:T(8,128)(2,1)S(1)} %get-tuple-element.80), channel_id=1, source_target_pairs={{0,8},{4,12},{8,0},{12,4},{1,9},{5,13},{9,1},{13,5},{2,10},{6,14},... | collective-permute-start | bytes 589832 | tf_op jit(solution)/shard_map/ppermute | solution.py:375
  79.3 9.0 %collective-permute-start.25 = (bf16[128,768]{1,0:T(8,128)(2,1)S(1)}, bf16[128,768]{1,0:T(8,128)(2,1)S(1)}, u32[]{:S(2)}, u32[]{:S(2)}) collective-permute-start(bf16[128,768]{1,0:T(8,128)(2,1)S(1)} %shard_map.78), channel_id=1, source_target_pairs={{0,3},{1,2},{2,1},{3,0},{4,7},{5,6},{6,5},{7,4},{8,11},{9,10},{10,... | collective-permute-start | bytes 589832 | tf_op jit(solution)/shard_map/ppermute | solution.py:378
  81.9 8.6 %collective-permute-start.28 = (bf16[128,768]{1,0:T(8,128)(2,1)S(1)}, bf16[128,768]{1,0:T(8,128)(2,1)S(1)}, u32[]{:S(2)}, u32[]{:S(2)}) collective-permute-start(bf16[128,768]{1,0:T(8,128)(2,1)S(1)} %shard_map.80), channel_id=1, source_target_pairs={{0,1},{1,0},{2,3},{3,2},{4,5},{5,4},{6,7},{7,6},{8,9},{9,8},{10,11... | collective-permute-start | bytes 589832 | tf_op jit(solution)/shard_map/ppermute | solution.py:378
